TPU v7x, 32 devices: a whole 2x2x4 slice. The times are simulated.
32 devices in a mesh: grp: 8 (over z, x), win: 4 (over y, core).
Axes of the slice: x: 2, y: 2, z: 4, core: 2. Of those that a mesh axis runs over, the one named last changes fastest.
Arguments:
- tokens: bfloat16 [32768, 128], P(('grp', 'win')), may hold values from -6 to 6
- positions: bfloat16 [2, 32768, 128], P(None, ('grp', 'win')), may hold values from -6 to 6
- cotangent: bfloat16 [32768, 128], P(('grp', 'win')), may hold values from -6 to 6
- route_send: int32 [2, 32768], P(None, ('grp', 'win')), may hold values from 0 to 2047, as said below
- recv_slot: int32 [2, 32, 2048], P(None, ('grp', 'win')), may hold values from 0 to 1728, as said below
- slot_bucket: int32 [2, 55296], P(None, ('grp', 'win')), may hold values from -1 to 3, as said below
- master: float32 [263936], P(('grp', 'win'))
- first_moment: float32 [263936], P(('grp', 'win'))
- second_moment: float32 [263936], P(('grp', 'win'))
Outputs:
- mixed: bfloat16 [32768, 128], P(('grp', 'win'))
- tokens_grad: float32 [32768, 128], P(('grp', 'win'))
- grad_norm: float32 [1], replicated
- clipped: float32 [263936], P(('grp', 'win'))
- new_master: float32 [263936], P(('grp', 'win'))
- new_first: float32 [263936], P(('grp', 'win'))
- new_second: float32 [263936], P(('grp', 'win'))
- new_copy: bfloat16 [263936], P(('grp', 'win'))
Inputs may be any that keep to these rules, and one draw needn't show every extreme that they name: `route_send`: the values of one device's pillars in one layer are distinct; a device sends at most 64 pillars to any one device, and in every draw some device sends exactly 64 to some device. `recv_slot`: for one layer and device the values below 1728 are distinct and name slots whose bucket id is not -1; every pillar that is sent gets a slot, and a device has at most 1408 occupied slots. `slot_bucket`: slots of one bucket lie in one aligned run of 144 slots; a run holds one bucket of 144, two of 60 or four of 30 slots, and unused slots; ids tell buckets of a run apart.
All inputs are finite; a program needn't handle non-finite values.
Results may differ from a plain program's by a relative error of at most 0.02.
The roundings to bfloat16 on the way count: a program that leaves them out, or rounds other values in their place, can miss the bound.
Values may be sent and summed in bfloat16 or wider, within the bound.
No kernel may reach another device: no remote copies, remote signals or barrier semaphores. Data moves between devices by JAX's collectives and lax.ppermute only.
A program may use at most 128 MiB of HBM per device.

v0:
```python
import math

import jax
import jax.numpy as jnp
from jax import lax
from jax.sharding import PartitionSpec as P

PILLAR_WIDTH = 128
FF = 256
HEAD_COUNT = 8
WINDOW_SLOTS = 144
LAYERS = 2
DEVICE_SLOTS = 1728
NPARAM = 263936


beta_one = 0.5
beta_two = 0.5
adam_step = 4
rate = 0.1
decay = 0.01
adam_eps = 1e-08


def norm_rows(value_rows, gain, shift):
    centre = value_rows - jnp.mean(value_rows, axis=-1, keepdims=True)
    spread = jnp.mean(centre * centre, axis=-1, keepdims=True)
    return centre * lax.rsqrt(spread + 1e-05) * gain + shift


def exact_gelu(value_rows):
    return jax.nn.gelu(value_rows, approximate=False)


def unpack(copies, layer_index):
    layer_size = 4 * PILLAR_WIDTH * PILLAR_WIDTH + 2 * PILLAR_WIDTH * FF + FF + 5 * PILLAR_WIDTH
    start = layer_index * layer_size
    shapes = [
        ("project_in", (PILLAR_WIDTH, 3 * PILLAR_WIDTH)),
        ("project_out", (PILLAR_WIDTH, PILLAR_WIDTH)),
        ("expand", (PILLAR_WIDTH, FF)),
        ("contract", (FF, PILLAR_WIDTH)),
        ("expand_bias", (FF,)),
        ("contract_bias", (PILLAR_WIDTH,)),
        ("gain_first", (PILLAR_WIDTH,)),
        ("shift_first", (PILLAR_WIDTH,)),
        ("gain_second", (PILLAR_WIDTH,)),
        ("shift_second", (PILLAR_WIDTH,)),
    ]
    params = {}
    for name, target_shape in shapes:
        count = math.prod(target_shape)
        params[name] = copies[start : start + count].reshape(target_shape)
        start = start + count
    return params


def deliver(buffer):
    groups = lax.axis_size("grp")
    windows = lax.axis_size("win")
    arrived_rows = lax.all_to_all(
        buffer.reshape((groups * windows, -1) + buffer.shape[1:]),
        ("grp", "win"),
        split_axis=0,
        concat_axis=0,
        tiled=True,
    )
    return arrived_rows.reshape(buffer.shape)


def inverse_tables(route, landing_slots):
    send_rows = landing_slots.shape[0]
    home_rows = route.shape[0]
    send_pick = (
        jnp.full((send_rows,), home_rows, jnp.int32)
        .at[route]
        .set(jnp.arange(home_rows, dtype=jnp.int32))
    )
    slot_pick = (
        jnp.full((DEVICE_SLOTS + 1,), send_rows, jnp.int32)
        .at[landing_slots]
        .set(jnp.arange(send_rows, dtype=jnp.int32))[:-1]
    )
    return (send_pick, slot_pick)


def with_blank(value_rows):
    return jnp.concatenate([value_rows, jnp.zeros((1,) + value_rows.shape[1:], value_rows.dtype)])


def to_owner(input_rows, tables):
    send_pick, slot_pick = tables
    buffer = jnp.take(with_blank(input_rows), send_pick, axis=0)
    arrived_rows = deliver(buffer)
    return jnp.take(with_blank(arrived_rows), slot_pick, axis=0)


def to_home(values, route, landing_slots):
    arrived_rows = deliver(jnp.take(with_blank(values), landing_slots, axis=0))
    return jnp.take(arrived_rows, route, axis=0)


def split_heads(value_rows):
    return value_rows.reshape(
        DEVICE_SLOTS // (4 * WINDOW_SLOTS), 4, WINDOW_SLOTS, HEAD_COUNT, PILLAR_WIDTH // HEAD_COUNT
    )


def masked_scores(query_block, key_block, bucket_block):
    scaling = float(query_block.shape[-1]) ** (-0.5)
    raw = (
        jnp.einsum("bqhd,bkhd->bhqk", query_block, key_block, preferred_element_type=jnp.float32)
        * scaling
    )
    same = (bucket_block[:, :, None] == bucket_block[:, None, :]) & (bucket_block[:, None, :] >= 0)
    return jnp.where(same[:, None], raw, -1e30)


def forward_group(stacked):
    query_block, key_block, value_block, bucket_block = stacked
    scores = masked_scores(query_block, key_block, bucket_block)
    highest = jnp.max(scores, axis=-1, keepdims=True)
    expos = jnp.exp(scores - highest)
    totals = jnp.sum(expos, axis=-1, keepdims=True)
    probs = (expos / totals).astype(jnp.bfloat16)
    final_result = jnp.einsum(
        "bhqk,bkhd->bqhd", probs, value_block, preferred_element_type=jnp.float32
    )
    return (final_result, (highest + jnp.log(totals))[..., 0])


def backward_group(stacked):
    query_block, key_block, value_block, bucket_block, log_totals, grad_block = stacked
    scaling = float(query_block.shape[-1]) ** (-0.5)
    scores = masked_scores(query_block, key_block, bucket_block)
    probs = jnp.exp(scores - log_totals[..., None])
    dprob = jnp.einsum(
        "bqhd,bkhd->bhqk", grad_block, value_block, preferred_element_type=jnp.float32
    )
    centre = jnp.sum(probs * dprob, axis=-1, keepdims=True)
    dscore = (probs * (dprob - centre)).astype(jnp.bfloat16)
    query_gradient = (
        jnp.einsum("bhqk,bkhd->bqhd", dscore, key_block, preferred_element_type=jnp.float32)
        * scaling
    )
    key_gradient = (
        jnp.einsum("bhqk,bqhd->bkhd", dscore, query_block, preferred_element_type=jnp.float32)
        * scaling
    )
    value_gradient = jnp.einsum(
        "bhqk,bqhd->bkhd",
        probs.astype(jnp.bfloat16),
        grad_block,
        preferred_element_type=jnp.float32,
    )
    return (query_gradient, key_gradient, value_gradient)


def attend(slot_rows, slot_pos, bucket_index, params):
    joined = (slot_rows.astype(jnp.float32) + slot_pos.astype(jnp.float32)).astype(jnp.bfloat16)
    query_key = jnp.dot(
        joined, params["project_in"][:, : 2 * PILLAR_WIDTH], preferred_element_type=jnp.float32
    ).astype(jnp.bfloat16)
    values = jnp.dot(
        slot_rows, params["project_in"][:, 2 * PILLAR_WIDTH :], preferred_element_type=jnp.float32
    ).astype(jnp.bfloat16)
    stacked = (
        split_heads(query_key[:, :PILLAR_WIDTH]),
        split_heads(query_key[:, PILLAR_WIDTH:]),
        split_heads(values),
        bucket_index.reshape(DEVICE_SLOTS // (4 * WINDOW_SLOTS), 4, WINDOW_SLOTS),
    )
    final_result, log_totals = lax.map(forward_group, stacked)
    live_mask = (bucket_index >= 0)[:, None]
    attended_output = jnp.where(
        live_mask, final_result.reshape(DEVICE_SLOTS, PILLAR_WIDTH), 0.0
    ).astype(jnp.bfloat16)
    branch = jnp.dot(
        attended_output, params["project_out"], preferred_element_type=jnp.float32
    ).astype(jnp.bfloat16)
    return {
        "joined": joined,
        "query_key": query_key,
        "values": values,
        "log_totals": log_totals,
        "attended": attended_output,
        "branch": branch,
    }


def owner_backward(owner, slot_rows, bucket_index, params, dbranch):
    dproject_out = jnp.einsum(
        "si,sj->ij", owner["attended"], dbranch, preferred_element_type=jnp.float32
    )
    live_mask = (bucket_index >= 0)[:, None]
    dattended = jnp.einsum(
        "sj,ij->si", dbranch, params["project_out"], preferred_element_type=jnp.float32
    )
    dattended = jnp.where(live_mask, dattended.astype(jnp.bfloat16), jnp.zeros((), jnp.bfloat16))
    query_key = owner["query_key"]
    stacked = (
        split_heads(query_key[:, :PILLAR_WIDTH]),
        split_heads(query_key[:, PILLAR_WIDTH:]),
        split_heads(owner["values"]),
        bucket_index.reshape(DEVICE_SLOTS // (4 * WINDOW_SLOTS), 4, WINDOW_SLOTS),
        owner["log_totals"],
        split_heads(dattended),
    )
    query_gradient, key_gradient, value_gradient = lax.map(backward_group, stacked)
    dquery_key = jnp.concatenate(
        [
            query_gradient.reshape(DEVICE_SLOTS, PILLAR_WIDTH),
            key_gradient.reshape(DEVICE_SLOTS, PILLAR_WIDTH),
        ],
        axis=1,
    ).astype(jnp.bfloat16)
    value_gradient = value_gradient.reshape(DEVICE_SLOTS, PILLAR_WIDTH).astype(jnp.bfloat16)
    dproject_in = jnp.concatenate(
        [
            jnp.einsum(
                "si,sj->ij", owner["joined"], dquery_key, preferred_element_type=jnp.float32
            ),
            jnp.einsum("si,sj->ij", slot_rows, value_gradient, preferred_element_type=jnp.float32),
        ],
        axis=1,
    )
    drows = jnp.einsum(
        "sj,ij->si",
        dquery_key,
        params["project_in"][:, : 2 * PILLAR_WIDTH],
        preferred_element_type=jnp.float32,
    ) + jnp.einsum(
        "sj,ij->si",
        value_gradient,
        params["project_in"][:, 2 * PILLAR_WIDTH :],
        preferred_element_type=jnp.float32,
    )
    return (dproject_in, dproject_out, drows.astype(jnp.bfloat16))


def home_forward(state, branch_home, params):
    resid = state.astype(jnp.float32) + branch_home.astype(jnp.float32)
    first = norm_rows(
        resid, params["gain_first"].astype(jnp.float32), params["shift_first"].astype(jnp.float32)
    )
    first_low = first.astype(jnp.bfloat16)
    inner = jnp.dot(first_low, params["expand"], preferred_element_type=jnp.float32) + params[
        "expand_bias"
    ].astype(jnp.float32)
    active = exact_gelu(inner).astype(jnp.bfloat16)
    outer = jnp.dot(active, params["contract"], preferred_element_type=jnp.float32) + params[
        "contract_bias"
    ].astype(jnp.float32)
    second = first + outer
    final_result = norm_rows(
        second,
        params["gain_second"].astype(jnp.float32),
        params["shift_second"].astype(jnp.float32),
    ).astype(jnp.bfloat16)
    return {
        "resid": resid,
        "first_low": first_low,
        "inner": inner,
        "active": active,
        "second": second,
        "result": final_result,
    }


def home_backward(home, params, grad_out):
    _, second_back = jax.vjp(
        norm_rows,
        home["second"],
        params["gain_second"].astype(jnp.float32),
        params["shift_second"].astype(jnp.float32),
    )
    dsecond, dgain_second, dshift_second = second_back(grad_out)
    douter = dsecond.astype(jnp.bfloat16)
    dcontract_bias = jnp.sum(douter.astype(jnp.float32), axis=0)
    dcontract = jnp.einsum("ti,tj->ij", home["active"], douter, preferred_element_type=jnp.float32)
    dactive = jnp.einsum(
        "tj,ij->ti", douter, params["contract"], preferred_element_type=jnp.float32
    )
    _, gelu_back = jax.vjp(exact_gelu, home["inner"])
    dinner = gelu_back(dactive)[0].astype(jnp.bfloat16)
    dexpand_bias = jnp.sum(dinner.astype(jnp.float32), axis=0)
    dexpand = jnp.einsum("ti,tj->ij", home["first_low"], dinner, preferred_element_type=jnp.float32)
    dfirst = (
        jnp.einsum("tj,ij->ti", dinner, params["expand"], preferred_element_type=jnp.float32)
        + dsecond
    )
    _, first_back = jax.vjp(
        norm_rows,
        home["resid"],
        params["gain_first"].astype(jnp.float32),
        params["shift_first"].astype(jnp.float32),
    )
    dresid, dgain_first, dshift_first = first_back(dfirst)
    small_grads = [
        dexpand_bias,
        dcontract_bias,
        dgain_first,
        dshift_first,
        dgain_second,
        dshift_second,
    ]
    return (dresid, dexpand, dcontract, small_grads)


def shards(
    tokens,
    positions,
    cotangent,
    route_send,
    recv_slot,
    slot_bucket,
    master,
    first_moment,
    second_moment,
):
    copies = lax.all_gather(master.astype(jnp.bfloat16), ("grp", "win"), axis=0, tiled=True)
    state = tokens
    records = []
    pickers = [
        inverse_tables(route_send[layer_index], recv_slot[layer_index, 0])
        for layer_index in range(LAYERS)
    ]
    for layer_index in range(LAYERS):
        params = unpack(copies, layer_index)
        route = route_send[layer_index]
        landing_slots = recv_slot[layer_index, 0]
        bucket_index = slot_bucket[layer_index]
        arrived_rows = to_owner(
            jnp.stack([state, positions[layer_index]], axis=1), pickers[layer_index]
        )
        owner = attend(arrived_rows[:, 0], arrived_rows[:, 1], bucket_index, params)
        home = home_forward(
            state, to_home(owner["branch"][:, None], route, landing_slots)[:, 0], params
        )
        records.append((state, None, None, home))
        state = home["result"]
    grad_out = cotangent.astype(jnp.float32)
    layer_grads = [None] * LAYERS
    for layer_index in reversed(range(LAYERS)):
        params = unpack(copies, layer_index)
        route = route_send[layer_index]
        landing_slots = recv_slot[layer_index, 0]
        bucket_index = slot_bucket[layer_index]
        layer_input, slot_rows, owner, home = records[layer_index]
        arrived_rows = to_owner(
            jnp.stack([layer_input, positions[layer_index]], axis=1), pickers[layer_index]
        )
        slot_rows = arrived_rows[:, 0]
        owner = attend(arrived_rows[:, 0], arrived_rows[:, 1], bucket_index, params)
        dresid, dexpand, dcontract, small_grads = home_backward(home, params, grad_out)
        dbranch = to_owner(dresid.astype(jnp.bfloat16)[:, None], pickers[layer_index])[:, 0]
        dproject_in, dproject_out, drows = owner_backward(
            owner, slot_rows, bucket_index, params, dbranch
        )
        grad_out = dresid + to_home(drows[:, None], route, landing_slots)[:, 0].astype(jnp.float32)
        layer_grads[layer_index] = jnp.concatenate(
            [
                dproject_in.reshape(-1),
                dproject_out.reshape(-1),
                dexpand.reshape(-1),
                dcontract.reshape(-1),
            ]
            + small_grads
        )
    flat_grad = jnp.concatenate(layer_grads)
    shard = lax.psum_scatter(flat_grad, ("grp", "win"), scatter_dimension=0, tiled=True)
    total = jnp.sqrt(lax.psum(jnp.sum(shard * shard), ("grp", "win")))
    clip_limit = 0.25 * math.sqrt(NPARAM)
    factor = jnp.minimum(1.0, clip_limit / (total + 1e-06))
    clipped = shard * factor
    new_first = beta_one * first_moment + (1.0 - beta_one) * clipped
    new_second = beta_two * second_moment + (1.0 - beta_two) * clipped * clipped
    first_hat = new_first / (1.0 - beta_one**adam_step)
    second_hat = new_second / (1.0 - beta_two**adam_step)
    new_master = master - rate * (first_hat / (jnp.sqrt(second_hat) + adam_eps) + decay * master)
    return (
        state,
        grad_out,
        total.reshape(1),
        clipped,
        new_master,
        new_first,
        new_second,
        new_master.astype(jnp.bfloat16),
    )


def solution(mesh):
    in_specs = (
        P(("grp", "win"), None),
        P(None, ("grp", "win"), None),
        P(("grp", "win"), None),
        P(None, ("grp", "win")),
        P(None, ("grp", "win"), None),
        P(None, ("grp", "win")),
        P(("grp", "win")),
        P(("grp", "win")),
        P(("grp", "win")),
    )
    out_specs = (
        P(("grp", "win"), None),
        P(("grp", "win"), None),
        P(),
        P(("grp", "win")),
        P(("grp", "win")),
        P(("grp", "win")),
        P(("grp", "win")),
        P(("grp", "win")),
    )
    return jax.shard_map(shards, mesh=mesh, in_specs=in_specs, out_specs=out_specs, check_vma=False)
```

profile of v0, /device:TPU:0, one launch (start us, length us, event | category | flops | bytes accessed | tf_op | source)
XLA Modules:
  0.0 855.8 jit_solution(1708372484940126660)
XLA Ops:
  21.8 7.0 gather_fusion
  28.9 8.2 broadcast_select_fusion.1
  37.0 7.3 all-to-all-start
  48.7 8.3 scatter_custom_fusion.1
  60.2 119.5 %all-reduce.17.cloned.1.call-done = bf16[263936]{0:T(1024)(128)(2,1)} async-done(((bf16[263936]{0:T(1024)(128)(2,1)}), bf16[263936]{0:T(1024)(128)(2,1)}) %all-reduce.17.cloned.1.call-update) | async-done | bytes 527888
  188.2 6.3 broadcast_select_fusion.3
  200.7 25.7 %while.72 = (s32[]{:T(128)}, bf16[3,4,144,8,16]{2,1,0,4,3:T(4,128)(2,1)S(1)}, bf16[3,4,144,8,16]{2,4,3,1,0:T(8,128)(2,1)S(1)}, s32[3,4,144]{2,1,0:T(4,128)}, bf1...) while((s32[]{:T(128)}, ...), condition=%wide.region_5.8_spmd, body=%wide.region_2.7_spmd.sunk | while | flops 46615248 | bytes 7043033 | solution.py:173
  230.6 7.3 gather_fusion.2
  249.2 11.2 %all-to-all-done.1 = bf16[32,64,1,128]{3,1,2,0:T(8,128)(2,1)S(1)} async-done(((bf16[32,64,1,128]{3,1,2,0:T(8,128)(2,1)}), bf16[32,64,1,128]{3,1,2,0:T(8,128)(2,1)S(1)}, u32[]{:S(2)}, u32[]{:S(2)}) %all-to-all-start.1) | async-done | bytes 524320 | tf_op jit(solution)/shard_map/all_to_all | solution.py:61
  272.4 7.0 gather_fusion.4
  279.4 8.2 broadcast_select_fusion
  290.8 8.7 %scatter_custom_fusion.3 = s32[1729]{0:T(1024)S(1)} fusion(s32[2048]{0:T(1024)} %bitcast.698, s32[2048]{0:T(1024)S(1)} %iota.15, s32[]{:T(128)} %constant.195.clone.1), kind=kCustom, calls=%fused_computation.450 | custom fusion | bytes 7428 | tf_op jit(solution)/shard_map/scatter | solution.py:82
  299.6 17.3 %all-to-all-done.2 = bf16[32,64,2,128]{3,2,1,0:T(2,128)(2,1)S(1)} async-done(((bf16[32,64,2,128]{3,2,1,0:T(2,128)(2,1)}), bf16[32,64,2,128]{3,2,1,0:T(2,128)(2,1)S(1)}, u32[]{:S(2)}, u32[]{:S(2)}) %all-to-all-start.2) | async-done | bytes 1048608 | tf_op jit(solution)/shard_map/all_to_all | solution.py:61
  323.7 6.3 broadcast_select_fusion.2
  339.1 23.7 %while.73 = (s32[]{:T(128)}, bf16[3,4,144,8,16]{2,1,0,4,3:T(4,128)(2,1)}, bf16[3,4,144,8,16]{2,4,3,1,0:T(8,128)(2,1)S(1)}, s32[3,4,144]{2,1,0:T(4,128)S(1)}, bf1...) while((s32[]{:T(128)}, ...), condition=%wide.region_15.20_spmd, body=%wide.region_12.19_spmd.sunk | while | flops 46615248 | bytes 6943189 | solution.py:173
  367.4 8.1 gather_fusion.6
  384.4 12.6 %all-to-all-done.3 = bf16[32,64,1,128]{3,1,2,0:T(8,128)(2,1)S(1)} async-done(((bf16[32,64,1,128]{3,1,2,0:T(8,128)(2,1)}), bf16[32,64,1,128]{3,1,2,0:T(8,128)(2,1)S(1)}, u32[]{:S(2)}, u32[]{:S(2)}) %all-to-all-start.3) | async-done | bytes 524320 | tf_op jit(solution)/shard_map/all_to_all | solution.py:61
  432.0 11.1 %while.74 = (s32[]{:T(128)}, bf16[3,4,144,8,16]{2,4,3,1,0:T(8,128)(2,1)S(1)}, f32[3,4,8,144]{3,2,1,0:T(8,128)S(1)}, bf16[3,4,144,8,16]{2,4,3,1,0:T(8,128)(2,1)S(...) while((s32[]{:T(128)}, ...), condition=%wide.region_27.32_spmd, body=%wide.region_24.31_spmd.sunk | while | flops 50591808 | bytes 12027869 | solution.py:173
  461.0 24.9 %while.75 = (s32[]{:T(128)}, bf16[3,4,144,8,16]{2,4,3,1,0:T(8,128)(2,1)}, bf16[3,4,144,8,16]{2,4,3,1,0:T(8,128)(2,1)}, bf16[3,4,144,8,16]{2,4,3,1,0:T(8,128)(2,1...) while((s32[]{:T(128)}, ...), condition=%wide.region_30.37_spmd, body=%wide.region_28.36_spmd.sunk | while | flops 116430912 | bytes 35252844 | solution.py:209
  504.9 14.0 %while.76 = (s32[]{:T(128)}, bf16[3,4,144,8,16]{2,4,3,1,0:T(8,128)(2,1)S(1)}, f32[3,4,8,144]{3,2,1,0:T(8,128)S(1)}, bf16[3,4,144,8,16]{2,4,3,1,0:T(8,128)(2,1)},...) while((s32[]{:T(128)}, ...), condition=%wide.region_38.45_spmd, body=%wide.region_35.44_spmd.sunk | while | flops 50591808 | bytes 12027869 | solution.py:173
  550.7 8.0 gather_fusion.12
  593.7 26.1 %while.77 = (s32[]{:T(128)}, bf16[3,4,144,8,16]{2,4,3,1,0:T(8,128)(2,1)S(1)}, bf16[3,4,144,8,16]{2,4,3,1,0:T(8,128)(2,1)}, bf16[3,4,144,8,16]{2,4,3,1,0:T(8,128)...) while((s32[]{:T(128)}, ...), condition=%wide.region_41.48_spmd, body=%wide.region_39.47_spmd.sunk | while | flops 116430912 | bytes 29456432 | solution.py:209
  667.4 131.2 %all-reduce.19.cloned.1.call-done = f32[263936]{0:T(1024)} async-done(((f32[263936]{0:T(1024)}), f32[263936]{0:T(1024)}) %all-reduce.19.cloned.1.call-update) | async-done | bytes 1055760
  800.0 40.8 %psum.7 = f32[]{:T(128)} all-reduce(f32[]{:T(128)} %multiply_reduce_fusion.12), channel_id=1, replica_groups=mesh['grp'=8,'win'=4] {'grp','win'}, use_global_device_ids=true, to_apply=%region_56.63 | all-reduce | flops 1 | bytes 8 | tf_op jit(solution)/shard_map/psum | solution.py:372
  (698 shorter events, 412.9 us)
Async XLA Ops:
  20.1 37.5 %copy-start.80 = (s32[2,1728]{1,0:T(2,128)S(1)}, s32[2,1728]{1,0:T(2,128)}, u32[]{:S(2)}) copy-start(s32[2,1728]{1,0:T(2,128)} %param.38) | copy-start | bytes 41476
  37.0 144.3 %all-to-all-start = ((bf16[32,64,2,128]{3,2,1,0:T(2,128)(2,1)}), bf16[32,64,2,128]{3,2,1,0:T(2,128)(2,1)S(1)}, u32[]{:S(2)}, u32[]{:S(2)}) async-start(bf16[32,64,2,128]{3,2,1,0:T(2,128)(2,1)} %bitcast.58), calls=%async_computation | async-start | bytes 2097152 | tf_op jit(solution)/shard_map/all_to_all | solution.py:61
  44.3 135.3 %all-reduce.17.cloned.1.call-start = ((), (), s32[]{:S(2)}) async-start(), calls=%async_computation.8 | async-start | bytes 1056768
  46.4 149.4 %copy-start.71 = (s32[1,1,2048]{2,1,0:T(1,128)}, s32[1,1,2048]{2,1,0:T(1,128)S(1)}, u32[]{:S(2)}) copy-start(s32[1,1,2048]{2,1,0:T(1,128)S(1)} %get-tuple-element.638) | copy-start | bytes 24580
  57.0 138.8 %copy-start.120 = (pred[1728]{0:T(1024)(128)(4,1)}, pred[1728]{0:T(1024)(128)(4,1)S(1)}, u32[]{:S(2)}) copy-start(pred[1728]{0:T(1024)(128)(4,1)S(1)} %compare_and_fusion.10) | copy-start | bytes 5188
  58.9 136.9 %copy-start.63 = (s32[2048]{0:T(1024)}, s32[2048]{0:T(1024)S(1)}, u32[]{:S(2)}) copy-start(s32[2048]{0:T(1024)S(1)} %pad_clamp_fusion.1) | copy-start | bytes 24580
  230.5 33.1 %copy-start.22 = (bf16[1024,128]{1,0:T(8,128)(2,1)S(1)}, bf16[1024,128]{1,0:T(8,128)(2,1)}, u32[]{:S(2)}) copy-start(bf16[1024,128]{1,0:T(8,128)(2,1)} %param.33) | copy-start | bytes 786436
  230.5 33.1 %copy-start.102 = (pred[1024]{0:T(1024)(128)(4,1)S(1)}, pred[1024]{0:T(1024)(128)(4,1)}, u32[]{:S(2)}) copy-start(pred[1024]{0:T(1024)(128)(4,1)} %compare_and_fusion.13) | copy-start | bytes 3076
  239.0 21.4 %all-to-all-start.1 = ((bf16[32,64,1,128]{3,1,2,0:T(8,128)(2,1)}), bf16[32,64,1,128]{3,1,2,0:T(8,128)(2,1)S(1)}, u32[]{:S(2)}, u32[]{:S(2)}) async-start(bf16[32,64,1,128]{3,1,2,0:T(8,128)(2,1)} %bitcast.67), calls=%async_computation.1 | async-start | bytes 1048576 | tf_op jit(solution)/shard_map/all_to_all | solution.py:61
  270.3 148.2 %copy-start = (f32[1024,128]{1,0:T(8,128)}, f32[1024,128]{1,0:T(8,128)S(1)}, u32[]{:S(2)}) copy-start(f32[1024,128]{1,0:T(8,128)S(1)} %get-tuple-element.648) | copy-start | bytes 1572868
  287.6 29.3 %all-to-all-start.2 = ((bf16[32,64,2,128]{3,2,1,0:T(2,128)(2,1)}), bf16[32,64,2,128]{3,2,1,0:T(2,128)(2,1)S(1)}, u32[]{:S(2)}, u32[]{:S(2)}) async-start(bf16[32,64,2,128]{3,2,1,0:T(2,128)(2,1)} %bitcast.81), calls=%async_computation.2 | async-start | bytes 2097152 | tf_op jit(solution)/shard_map/all_to_all | solution.py:61
  299.6 32.1 %copy-start.42 = (bf16[128,384]{1,0:T(8,128)(2,1)}, bf16[128,384]{1,0:T(8,128)(2,1)S(1)}, u32[]{:S(2)}) copy-start(bf16[128,384]{1,0:T(8,128)(2,1)S(1)} %reshape.782) | copy-start | bytes 294916
  377.6 19.3 %all-to-all-start.3 = ((bf16[32,64,1,128]{3,1,2,0:T(8,128)(2,1)}), bf16[32,64,1,128]{3,1,2,0:T(8,128)(2,1)S(1)}, u32[]{:S(2)}, u32[]{:S(2)}) async-start(bf16[32,64,1,128]{3,1,2,0:T(8,128)(2,1)} %bitcast.687), calls=%async_computation.3 | async-start | bytes 1048576 | tf_op jit(solution)/shard_map/all_to_all | solution.py:61
  381.4 37.1 %copy-start.81 = (pred[1024]{0:T(1024)(128)(4,1)}, pred[1024]{0:T(1024)(128)(4,1)S(1)}, u32[]{:S(2)}) copy-start(pred[1024]{0:T(1024)(128)(4,1)S(1)} %compare_and_fusion.12) | copy-start | bytes 3076
  428.2 19.3 %all-to-all-start.4 = ((bf16[32,64,1,128]{3,1,2,0:T(8,128)(2,1)}), bf16[32,64,1,128]{3,1,2,0:T(8,128)(2,1)}, u32[]{:S(2)}, u32[]{:S(2)}) async-start(bf16[32,64,1,128]{3,1,2,0:T(8,128)(2,1)} %bitcast.685), calls=%async_computation.4 | async-start | bytes 1048576 | tf_op jit(solution)/shard_map/all_to_all | solution.py:61
  501.6 31.8 %all-to-all-start.5 = ((bf16[32,64,1,128]{3,1,2,0:T(8,128)(2,1)}), bf16[32,64,1,128]{3,1,2,0:T(8,128)(2,1)S(1)}, u32[]{:S(2)}, u32[]{:S(2)}) async-start(bf16[32,64,1,128]{3,1,2,0:T(8,128)(2,1)} %bitcast.109), calls=%async_computation.5 | async-start | bytes 1048576 | tf_op jit(solution)/shard_map/all_to_all | solution.py:61
  560.9 21.6 %all-to-all-start.6 = ((bf16[32,64,1,128]{3,1,2,0:T(8,128)(2,1)}), bf16[32,64,1,128]{3,1,2,0:T(8,128)(2,1)}, u32[]{:S(2)}, u32[]{:S(2)}) async-start(bf16[32,64,1,128]{3,1,2,0:T(8,128)(2,1)} %bitcast.686), calls=%async_computation.6 | async-start | bytes 1048576 | tf_op jit(solution)/shard_map/all_to_all | solution.py:61
  634.9 206.6 %copy-start.62 = (f32[8248]{0:T(1024)S(1)}, f32[8248]{0:T(1024)}, u32[]{:S(2)}) copy-start(f32[8248]{0:T(1024)} %param.39) | copy-start | bytes 98980
  634.9 206.6 %copy-start.95 = (f32[8248]{0:T(1024)S(1)}, f32[8248]{0:T(1024)}, u32[]{:S(2)}) copy-start(f32[8248]{0:T(1024)} %param.40) | copy-start | bytes 98980
  635.0 206.6 %copy-start.96 = (f32[8248]{0:T(1024)S(1)}, f32[8248]{0:T(1024)}, u32[]{:S(2)}) copy-start(f32[8248]{0:T(1024)} %param.41) | copy-start | bytes 98980
  635.0 208.1 %copy-start.84 = (s32[1024]{0:T(1024)S(1)}, s32[1024]{0:T(1024)}, u32[]{:S(2)}) copy-start(s32[1024]{0:T(1024)} %fusion.244) | copy-start | bytes 12292
  635.0 211.3 %copy-start.19 = (f32[1024,128]{1,0:T(8,128)S(1)}, f32[1024,128]{1,0:T(8,128)}, u32[]{:S(2)}) copy-start(f32[1024,128]{1,0:T(8,128)} %copy-done.18) | copy-start | bytes 1572868
  642.4 200.7 %all-to-all-start.7 = ((bf16[32,64,1,128]{3,1,2,0:T(8,128)(2,1)}), bf16[32,64,1,128]{3,1,2,0:T(8,128)(2,1)S(1)}, u32[]{:S(2)}, u32[]{:S(2)}) async-start(bf16[32,64,1,128]{3,1,2,0:T(8,128)(2,1)} %bitcast.127), calls=%async_computation.7 | async-start | bytes 1048576 | tf_op jit(solution)/shard_map/all_to_all | solution.py:61
  645.4 153.1 %all-reduce.19.cloned.1.call-start = ((), (), s32[]{:S(2)}) async-start(), calls=%async_computation.9 | async-start | bytes 2113536
  (147 other events, 1733.6 us)
Sparse Core Ops, SparseCore 0:
  50.4 129.2 all-reduce.16
  667.5 130.9 all-reduce.18
where the time goes:
time: 865 us; the launch traced here: 856 us
  waiting for transfers between devices  299 us (35%)
  local copies, waits for them, and re-layouts  220 us (25%)
  matrix products  141 us (16%)
  other arithmetic  98.8 us (11%)
  blocking collectives  40.8 us (5%)
  starting transfers between devices  36.1 us (4%)
  between operations  19 us (2%)
    unnamed x4, waiting for transfers between devices  251 us
    all_to_all x8, waiting for transfers between devices, deliver(): lax.all_to_all(buffer.reshape((groups * windows, -1) + buffer.shape[1:]),...  48.6 us
    psum x1, blocking collectives, shards(): total = jnp.sqrt(lax.psum(jnp.sum(shard * shard), ('grp', 'win')))  40.8 us
    all_to_all x8, starting transfers between devices, deliver(): lax.all_to_all(buffer.reshape((groups * windows, -1) + buffer.shape[1:]),...  36 us
    unnamed x312, local copies, waits for them, and re-layouts  33.6 us
    gather x4, local copies, waits for them, and re-layouts, to_owner(): buffer = jnp.take(with_blank(input_rows), send_pick, axis=0)  28.2 us
    gather x4, local copies, waits for them, and re-layouts, to_home(): arrived_rows = deliver(jnp.take(with_blank(values), landing_slots, axis=0))  27.7 us
    dot_general x12, matrix products, forward_group(): jnp.einsum('bhqk,bkhd->bqhd', probs, value_block, preferred_element_type=...  26.9 us
  transfers between devices with their start and end apart: 10, of which 7 were waited for; matrix products, arithmetic and copies ran while one was open for 13% of the time, Pallas kernels for 0%

commit v1 on v0

v1 whole, which is shorter than its diff:
```python
import functools
import math

import jax
import jax.numpy as jnp
from jax import lax
from jax.experimental import pallas as pl
from jax.experimental.pallas import tpu as pltpu
from jax.sharding import PartitionSpec as P

PILLAR_WIDTH = 128
FF = 256
HEAD_COUNT = 8
HDIM = 16
WINDOW_SLOTS = 144
LAYERS = 2
DEVICE_SLOTS = 1728
NSUB = 12
NPARAM = 263936
LAYER_ROWS = 1031
EXPANDED = HEAD_COUNT * WINDOW_SLOTS
MASKED = -1e30
LOWEST = -3e38

beta_one = 0.5
beta_two = 0.5
adam_step = 4
rate = 0.1
decay = 0.01
adam_eps = 1e-08

BF16 = jnp.bfloat16
F32 = jnp.float32
AXES = ("grp", "win")
PARAMS = pltpu.CompilerParams(vmem_limit_bytes=48 << 20)

NN = (((1,), (0,)), ((), ()))
NT = (((1,), (1,)), ((), ()))
TN = (((0,), (0,)), ((), ()))


def mm(left, right, dims=NN):
    return lax.dot_general(left, right, dims, preferred_element_type=F32)


def iota(shape, dim):
    return lax.broadcasted_iota(jnp.int32, shape, dim)


def shape_of(shape, dtype):
    return jax.ShapeDtypeStruct(shape, dtype)


def one_hot_rows(row_ids, first, count):
    return jnp.where(iota((count, row_ids.shape[1]), 0) + first == row_ids, 1.0, 0.0).astype(BF16)


def one_hot_columns(column_ids, width):
    lane = iota(column_ids.shape, 1)
    pieces = [
        jnp.where(column_ids == lane + 128 * k, 1.0, 0.0).astype(BF16)
        for k in range(-(-width // 128))
    ]
    return jnp.concatenate(pieces, axis=1)[:, :width]


def expand_heads(block, heads):
    main = block[:128]
    tail = block[128:]
    return jnp.concatenate([main] * HEAD_COUNT + [tail] * HEAD_COUNT, axis=0) * heads


def scatter_rows(route_row, low_rows, send, chunk=256):
    for c in range(send.shape[0] // chunk):
        hot = one_hot_rows(route_row, c * chunk, chunk)
        send[c * chunk : (c + 1) * chunk, :] = mm(hot, low_rows).astype(BF16)


def land_rows(recv_col, slot_values, send, chunk=128):
    for c in range(send.shape[0] // chunk):
        part = slice(c * chunk, (c + 1) * chunk)
        hot = one_hot_columns(recv_col[part, :], DEVICE_SLOTS)
        send[part, :] = mm(hot, slot_values).astype(BF16)


def start_kernel(route_ref, tokens_ref, pos_ref, out_ref, out_next_ref):
    both = jnp.concatenate([tokens_ref[...], pos_ref[0]], axis=1)
    scatter_rows(route_ref[0:1, :], both, out_ref)
    scatter_rows(route_ref[1:2, :], pos_ref[1], out_next_ref)


def owner_forward_kernel(
    recv_ref,
    recv_col_ref,
    bucket_ref,
    heads_ref,
    win_ref,
    wout_ref,
    rows_ref,
    pos_ref,
    send_ref,
    kept_ref,
    qkv_ref,
    expo_ref,
    out_ref,
    total_ref,
    branch_ref,
):
    def one_run(run, carry):
        base = pl.multiple_of(run * WINDOW_SLOTS, 16)
        here = pl.ds(base, WINDOW_SLOTS)
        hot = one_hot_rows(recv_ref[...], base, WINDOW_SLOTS)
        if pos_ref is None:
            landed = mm(hot, rows_ref[...])
        else:
            landed = mm(hot, jnp.concatenate([rows_ref[...], pos_ref[...]], axis=1))
        slot_rows = landed[:, :128].astype(BF16)
        joined = (landed[:, :128] + landed[:, 128:]).astype(BF16)
        query_key = mm(joined, win_ref[:, :256]).astype(BF16)
        values = mm(slot_rows, win_ref[:, 256:]).astype(BF16)
        kept_ref[here, :] = jnp.concatenate([joined, slot_rows], axis=1)
        qkv_ref[here, :] = jnp.concatenate([query_key, values], axis=1)
        heads = heads_ref[...]
        bucket = bucket_ref[here, :]
        lane = iota((WINDOW_SLOTS, 128), 1)
        own = jnp.where(bucket == lane, 1.0, 0.0).astype(BF16)
        other = jnp.where((lane < 4) & (bucket != lane), MASKED, 0.0).astype(BF16)
        queries = (query_key[:, :128].astype(F32) * 0.25).astype(BF16)
        query_wide = jnp.concatenate([queries, own], axis=1)
        others = jnp.concatenate([other[:128]] * 8 + [other[128:]] * 8, axis=0)
        key_wide = jnp.concatenate([expand_heads(query_key[:, 128:], heads), others], axis=1)
        scores = mm(query_wide, key_wide, NT)
        tail = scores[:, 1024:]
        segment = lane >> 4
        tail_top = jnp.zeros((WINDOW_SLOTS, 128), F32)
        pieces = []
        for h in range(HEAD_COUNT):
            main = scores[:, 128 * h : 128 * h + 128]
            mine = segment == h
            top = jnp.max(
                jnp.maximum(main, jnp.where(mine, tail, LOWEST)), axis=1, keepdims=True
            )
            tail_top = jnp.where(mine, top, tail_top)
            pieces.append(jnp.exp(main - top).astype(BF16))
        pieces.append(jnp.exp(tail - tail_top).astype(BF16))
        expo = jnp.concatenate(pieces, axis=1)
        expo_ref[here, :] = expo
        value_wide = jnp.concatenate([expand_heads(values, heads), heads], axis=1)
        summed = mm(expo, value_wide)
        total = summed[:, 128:]
        attended = summed[:, :128] / total
        out_ref[here, :] = attended
        total_ref[here, :] = total
        attended = jnp.where(bucket >= 0, attended, 0.0).astype(BF16)
        branch_ref[here, :] = mm(attended, wout_ref[...]).astype(BF16)
        return carry

    lax.fori_loop(0, NSUB, one_run, 0)
    land_rows(recv_col_ref, branch_ref[...], send_ref)


def owner_backward_kernel(
    recv_ref,
    recv_col_ref,
    bucket_ref,
    heads_ref,
    unfold_ref,
    win_ref,
    wout_ref,
    grads_ref,
    kept_ref,
    qkv_ref,
    expo_ref,
    out_ref,
    total_ref,
    send_ref,
    dwin_ref,
    dwout_ref,
    attended_ref,
    dbranch_ref,
    dqkv_ref,
):
    def one_run(run, carry):
        base = pl.multiple_of(run * WINDOW_SLOTS, 16)
        here = pl.ds(base, WINDOW_SLOTS)
        heads = heads_ref[...]
        block = heads[1024:]
        hot = one_hot_rows(recv_ref[...], base, WINDOW_SLOTS)
        dbranch = mm(hot, grads_ref[...]).astype(BF16)
        live = bucket_ref[here, :] >= 0
        out = out_ref[here, :]
        attended_ref[here, :] = jnp.where(live, out, 0.0).astype(BF16)
        dbranch_ref[here, :] = dbranch
        dattended = mm(dbranch, wout_ref[...], NT).astype(BF16).astype(F32)
        dout = (jnp.where(live, dattended, 0.0) / total_ref[here, :]).astype(BF16)
        weighed = dout.astype(F32) * out
        weighed_high = weighed.astype(BF16)
        weighed_low = (weighed - weighed_high.astype(F32)).astype(BF16)
        centre = mm(weighed_high, block) + mm(weighed_low, block)
        centre_high = centre.astype(BF16).astype(F32)
        place = iota((WINDOW_SLOTS, 128), 1) & 15
        aside = jnp.where(
            place == 0, -centre_high, jnp.where(place == 1, centre_high - centre, 0.0)
        ).astype(BF16)
        dout_wide = jnp.concatenate([dout, aside], axis=1)
        queries = qkv_ref[here, 0:128]
        keys_wide = expand_heads(qkv_ref[here, 128:256], heads)
        value_wide = jnp.concatenate([expand_heads(qkv_ref[here, 256:384], heads), heads], axis=1)
        expo = expo_ref[here, :]
        dscore = (mm(dout_wide, value_wide, NT) * expo.astype(F32)).astype(BF16)
        dqueries = (mm(dscore, keys_wide) * 0.25).astype(BF16)

        def gathered(left, right, scale):
            wide = mm(left, right, TN)
            main = jnp.concatenate(
                [wide[16 * h : 16 * h + 16, 128 * h : 128 * h + 128] for h in range(HEAD_COUNT)],
                axis=0,
            )
            tail = wide[:, 1024:] * block.astype(F32)
            folded = (jnp.concatenate([main, tail], axis=1) * scale).astype(BF16)
            return mm(unfold_ref[...], folded, NT).astype(BF16)

        dkeys = gathered(queries, dscore, 0.25)
        dvalues = gathered(dout, expo, 1.0)
        dqkv_ref[here, :] = jnp.concatenate([dqueries, dkeys, dvalues], axis=1)
        return carry

    lax.fori_loop(0, NSUB, one_run, 0)
    dwout_ref[...] = mm(attended_ref[...], dbranch_ref[...], TN)
    dqkv = dqkv_ref[...]
    kept = kept_ref[...]
    dwin_ref[:, :256] = mm(kept[:, :128], dqkv[:, :256], TN)
    dwin_ref[:, 256:] = mm(kept[:, 128:], dqkv[:, 256:], TN)
    drows = mm(dqkv, win_ref[...], NT).astype(BF16)
    land_rows(recv_col_ref, drows, send_ref)


def centred_rows(rows):
    centre = rows - jnp.mean(rows, axis=-1, keepdims=True)
    spread = jnp.mean(centre * centre, axis=-1, keepdims=True)
    inverse = lax.rsqrt(spread + 1e-05)
    return centre * inverse, inverse


def norm_back(grad, gain, unit, inverse):
    dunit = grad * gain
    return (
        dunit
        - jnp.mean(dunit, axis=-1, keepdims=True)
        - unit * jnp.mean(dunit * unit, axis=-1, keepdims=True)
    ) * inverse


def feed_forward(resid, expand, contract, vecs):
    unit, inverse = centred_rows(resid)
    first = unit * vecs[3:4, :] + vecs[4:5, :]
    first_low = first.astype(BF16)
    bias = jnp.concatenate([vecs[0:1, :], vecs[1:2, :]], axis=1)
    inner = mm(first_low, expand) + bias
    below = 0.5 + 0.5 * lax.erf(inner * math.sqrt(0.5))
    active = (inner * below).astype(BF16)
    second = first + (mm(active, contract) + vecs[2:3, :])
    return unit, inverse, first_low, inner, below, active, second


ROWS = 128


def home_forward_kernel(
    route_col_ref,
    route_ref,
    branch_ref,
    state_ref,
    expand_ref,
    contract_ref,
    vecs_ref,
    result_ref,
    send_ref,
    resid_ref,
):
    def some_rows(c, carry):
        here = pl.ds(pl.multiple_of(c * ROWS, ROWS), ROWS)
        vecs = vecs_ref[...]
        hot = one_hot_columns(route_col_ref[here, :], branch_ref.shape[0])
        resid = state_ref[here, :].astype(F32) + mm(hot, branch_ref[...])
        resid_ref[here, :] = resid
        second = feed_forward(resid, expand_ref[...], contract_ref[...], vecs)[-1]
        unit, _ = centred_rows(second)
        result_ref[here, :] = (unit * vecs[5:6, :] + vecs[6:7, :]).astype(BF16)
        return carry

    lax.fori_loop(0, result_ref.shape[0] // ROWS, some_rows, 0)
    scatter_rows(route_ref[...], result_ref[...], send_ref)


def home_backward_kernel(
    top,
    route_col_ref,
    route_ref,
    arrived_ref,
    base_ref,
    cotangent_ref,
    expand_ref,
    contract_ref,
    vecs_ref,
    *rest,
):
    if top:
        result_ref, *rest = rest
    (
        dresid_ref,
        send_ref,
        dexpand_ref,
        dcontract_ref,
        dvecs_ref,
        active_ref,
        douter_ref,
        first_ref,
        dinner_ref,
        low_ref,
    ) = rest
    dvecs_ref[...] = jnp.zeros_like(dvecs_ref)

    def some_rows(c, carry):
        here = pl.ds(pl.multiple_of(c * ROWS, ROWS), ROWS)
        vecs = vecs_ref[...]
        expand = expand_ref[...]
        contract = contract_ref[...]
        hot = one_hot_columns(route_col_ref[here, :], arrived_ref.shape[0])
        taken = mm(hot, arrived_ref[...])
        if top:
            resid = base_ref[here, :].astype(F32) + taken
            grad = cotangent_ref[here, :].astype(F32)
        else:
            resid = base_ref[here, :]
            grad = cotangent_ref[here, :] + taken
        unit_first, inverse_first, first_low, inner, below, active, second = feed_forward(
            resid, expand, contract, vecs
        )
        unit, inverse = centred_rows(second)
        if top:
            result_ref[here, :] = (unit * vecs[5:6, :] + vecs[6:7, :]).astype(BF16)
        dsecond = norm_back(grad, vecs[5:6, :], unit, inverse)
        douter = dsecond.astype(BF16)
        slope = below + inner * (jnp.exp(-0.5 * inner * inner) * (1.0 / math.sqrt(2.0 * math.pi)))
        dinner = (mm(douter, contract, NT) * slope).astype(BF16)
        dfirst = mm(dinner, expand, NT) + dsecond
        dresid = norm_back(dfirst, vecs[3:4, :], unit_first, inverse_first)
        dresid_ref[here, :] = dresid
        low_ref[here, :] = dresid.astype(BF16)
        active_ref[here, :] = active
        douter_ref[here, :] = douter
        first_ref[here, :] = first_low
        dinner_ref[here, :] = dinner

        def down(rows):
            return jnp.sum(rows, axis=0, keepdims=True)

        dbias = down(dinner.astype(F32))
        dvecs_ref[...] += jnp.concatenate(
            [
                dbias[:, :128],
                dbias[:, 128:],
                down(douter.astype(F32)),
                down(dfirst * unit_first),
                down(dfirst),
                down(grad * unit),
                down(grad),
                jnp.zeros((1, 128), F32),
            ],
            axis=0,
        )
        return carry

    lax.fori_loop(0, dresid_ref.shape[0] // ROWS, some_rows, 0)
    scatter_rows(route_ref[...], low_ref[...], send_ref)
    dcontract_ref[...] = mm(active_ref[...], douter_ref[...], TN)
    dexpand_ref[...] = mm(first_ref[...], dinner_ref[...], TN)


def finish_kernel(route_col_ref, arrived_ref, dresid_ref, out_ref):
    for c in range(out_ref.shape[0] // ROWS):
        part = slice(c * ROWS, (c + 1) * ROWS)
        hot = one_hot_columns(route_col_ref[part, :], arrived_ref.shape[0])
        out_ref[part, :] = dresid_ref[part, :] + mm(hot, arrived_ref[...])


def unpack_kernel(order, share, block_rows, shards_ref, *rest):
    flat_ref = rest[-1]
    outs = rest[:-1]
    lane = iota((block_rows, 128), 1)
    for device, place in enumerate(order):
        row, shift = divmod(device * share, 128)
        block = shards_ref[place].astype(F32)
        if shift:
            block = pltpu.roll(block, shift, 1)
            before = jnp.concatenate([flat_ref[pl.ds(row, 1), :], block[:-1]], axis=0)
            block = jnp.where(lane >= shift, block, before)
        flat_ref[pl.ds(row, block_rows), :] = block
    for layer in range(LAYERS):
        win_ref, wout_ref, expand_ref, contract_ref, vecs_ref = outs[5 * layer : 5 * layer + 5]
        base = layer * LAYER_ROWS
        for j in range(3):
            win_ref[:, 128 * j : 128 * j + 128] = flat_ref[pl.ds(base + j, 128, stride=3), :].astype(
                BF16
            )
        wout_ref[...] = flat_ref[pl.ds(base + 384, 128), :].astype(BF16)
        for j in range(2):
            expand_ref[:, 128 * j : 128 * j + 128] = flat_ref[
                pl.ds(base + 512 + j, 128, stride=2), :
            ].astype(BF16)
        contract_ref[...] = flat_ref[pl.ds(base + 768, 256), :].astype(BF16)
        vecs_ref[0:7, :] = flat_ref[pl.ds(base + 1024, 7), :]
        vecs_ref[7:8, :] = jnp.zeros((1, 128), F32)


def pack_kernel(devices, share, block_rows, *refs):
    flat_ref = refs[-1]
    out_ref = refs[-2]
    for layer in range(LAYERS):
        dwin_ref, dwout_ref, dexpand_ref, dcontract_ref, dvecs_ref = refs[5 * layer : 5 * layer + 5]
        base = layer * LAYER_ROWS
        for j in range(3):
            flat_ref[pl.ds(base + j, 128, stride=3), :] = dwin_ref[:, 128 * j : 128 * j + 128]
        flat_ref[pl.ds(base + 384, 128), :] = dwout_ref[...]
        for j in range(2):
            flat_ref[pl.ds(base + 512 + j, 128, stride=2), :] = dexpand_ref[
                :, 128 * j : 128 * j + 128
            ]
        flat_ref[pl.ds(base + 768, 256), :] = dcontract_ref[...]
        flat_ref[pl.ds(base + 1024, 7), :] = dvecs_ref[0:7, :]
    end = LAYERS * LAYER_ROWS
    flat_ref[pl.ds(end, flat_ref.shape[0] - end), :] = jnp.zeros(
        (flat_ref.shape[0] - end, 128), F32
    )
    lane = iota((block_rows, 128), 1)
    for device in range(devices):
        row, shift = divmod(device * share, 128)
        block = flat_ref[pl.ds(row, block_rows), :]
        if shift:
            after = flat_ref[pl.ds(row + 1, block_rows), :]
            block = pltpu.roll(jnp.where(lane >= shift, block, after), 128 - shift, 1)
        out_ref[device] = block.astype(BF16)


def call(body, outs, *args, scratch=()):
    return pl.pallas_call(
        body,
        out_shape=tuple(shape_of(s, d) for s, d in outs),
        scratch_shapes=[pltpu.VMEM(s, d) for s, d in scratch],
        compiler_params=PARAMS,
    )(*args)


def exchange(buffer, axes=AXES):
    return lax.all_to_all(buffer, axes, split_axis=0, concat_axis=0, tiled=True)


def on_lanes(ids):
    return jnp.broadcast_to(ids[:, None], (ids.shape[0], 128))


def shards(
    tokens,
    positions,
    cotangent,
    route_send,
    recv_slot,
    slot_bucket,
    master,
    first_moment,
    second_moment,
):
    groups = lax.axis_size("grp")
    windows = lax.axis_size("win")
    devices = groups * windows
    home = tokens.shape[0]
    arrivals = recv_slot.shape[2]
    share = master.shape[0]
    block_rows = -(-share // 128)
    block_rows = -(-block_rows // 16) * 16
    width = PILLAR_WIDTH

    heads_id = jnp.concatenate(
        [jnp.arange(1024, dtype=jnp.int32) // 128, jnp.arange(128, dtype=jnp.int32) // 16]
    )
    lane = jnp.arange(128, dtype=jnp.int32)
    heads = (heads_id[:, None] == lane[None, :] // 16).astype(BF16)
    slot = jnp.arange(WINDOW_SLOTS, dtype=jnp.int32)
    wide = jnp.arange(256, dtype=jnp.int32)
    wide = jnp.where(wide < 128, wide, 128 + wide % 16)
    unfold = (slot[:, None] == wide[None, :]).astype(BF16)

    mine = jnp.pad(master.astype(BF16), (0, block_rows * 128 - share)).reshape(1, block_rows, 128)
    copies = exchange(jnp.broadcast_to(mine, (groups, block_rows, 128)), "grp")
    copies = exchange(
        jnp.broadcast_to(copies[None], (windows, groups, block_rows, 128)).reshape(
            devices, block_rows, 128
        ),
        "win",
    )
    order = [(d % windows) * groups + d // windows for d in range(devices)]
    flat_rows = -(-(((devices - 1) * share) // 128 + block_rows + 8) // 8) * 8
    layer_shapes = (
        ((width, 3 * width), BF16),
        ((width, width), BF16),
        ((width, FF), BF16),
        ((FF, width), BF16),
        ((8, width), F32),
    )
    params = call(
        functools.partial(unpack_kernel, order, share, block_rows),
        layer_shapes * LAYERS,
        copies,
        scratch=(((flat_rows, 128), F32),),
    )
    params = [params[5 * l : 5 * l + 5] for l in range(LAYERS)]

    send, send_next = call(
        start_kernel,
        (((arrivals, 2 * width), BF16), ((arrivals, width), BF16)),
        route_send,
        tokens,
        positions,
    )
    arrived = exchange(send)
    pos_next = exchange(send_next)

    recv = [recv_slot[l] for l in range(LAYERS)]
    recv_col = [on_lanes(recv_slot[l, 0]) for l in range(LAYERS)]
    route = [route_send[l : l + 1] for l in range(LAYERS)]
    route_col = [on_lanes(route_send[l]) for l in range(LAYERS)]
    bucket = [on_lanes(slot_bucket[l]) for l in range(LAYERS)]

    def owner_forward(layer, rows, pos):
        win, wout = params[layer][:2]
        args = [recv[layer], recv_col[layer], bucket[layer], heads, win, wout, rows]
        if pos is None:
            body = lambda *refs: owner_forward_kernel(*refs[:7], None, *refs[7:])
        else:
            body = owner_forward_kernel
            args.append(pos)
        return call(
            body,
            (
                ((arrivals, width), BF16),
                ((DEVICE_SLOTS, 2 * width), BF16),
                ((DEVICE_SLOTS, 3 * width), BF16),
                ((DEVICE_SLOTS, EXPANDED), BF16),
                ((DEVICE_SLOTS, width), F32),
                ((DEVICE_SLOTS, width), F32),
            ),
            *args,
            scratch=(((DEVICE_SLOTS, width), BF16),),
        )

    def owner_backward(layer, grads, kept):
        win, wout = params[layer][:2]
        return call(
            owner_backward_kernel,
            (
                ((arrivals, width), BF16),
                ((width, 3 * width), F32),
                ((width, width), F32),
            ),
            recv[layer],
            recv_col[layer],
            bucket[layer],
            heads,
            unfold,
            win,
            wout,
            grads,
            *kept,
            scratch=(
                ((DEVICE_SLOTS, width), BF16),
                ((DEVICE_SLOTS, width), BF16),
                ((DEVICE_SLOTS, 3 * width), BF16),
            ),
        )

    def home_backward(layer, top, arrived_rows, base, grad):
        outs = (
            ((home, width), F32),
            ((arrivals, width), BF16),
            ((width, FF), F32),
            ((FF, width), F32),
            ((8, width), F32),
        )
        if top:
            outs = (((home, width), BF16),) + outs
        return call(
            functools.partial(home_backward_kernel, top),
            outs,
            route_col[1],
            route[layer],
            arrived_rows,
            base,
            grad,
            *params[layer][2:],
            scratch=(
                ((home, FF), BF16),
                ((home, width), BF16),
                ((home, width), BF16),
                ((home, FF), BF16),
                ((home, width), BF16),
            ),
        )

    send, *kept_zero = owner_forward(0, arrived, None)
    state, send, resid_zero = call(
        home_forward_kernel,
        (((home, width), BF16), ((arrivals, width), BF16), ((home, width), F32)),
        route_col[0],
        route[1],
        exchange(send),
        tokens,
        *params[0][2:],
    )
    send, *kept_one = owner_forward(1, exchange(send), pos_next)
    mixed, dresid, send, *ffn_one = home_backward(1, True, exchange(send), state, cotangent)
    send, *att_one = owner_backward(1, exchange(send), kept_one)
    dresid, send, *ffn_zero = home_backward(0, False, exchange(send), resid_zero, dresid)
    send, *att_zero = owner_backward(0, exchange(send), kept_zero)
    (tokens_grad,) = call(
        finish_kernel, (((home, width), F32),), route_col[0], exchange(send), dresid
    )

    (packed,) = call(
        functools.partial(pack_kernel, devices, share, block_rows),
        (((devices, block_rows, 128), BF16),),
        *att_zero,
        *ffn_zero,
        *att_one,
        *ffn_one,
        scratch=(((flat_rows, 128), F32),),
    )
    shard = jnp.sum(exchange(packed).astype(F32), axis=0).reshape(-1)[:share]
    partial_square = jnp.broadcast_to(jnp.sum(shard * shard), (devices, 8, 128))
    total = jnp.sqrt(jnp.sum(exchange(partial_square)[:, 0, 0]))
    clip_limit = 0.25 * math.sqrt(NPARAM)
    factor = jnp.minimum(1.0, clip_limit / (total + 1e-06))
    clipped = shard * factor
    new_first = beta_one * first_moment + (1.0 - beta_one) * clipped
    new_second = beta_two * second_moment + (1.0 - beta_two) * clipped * clipped
    first_hat = new_first / (1.0 - beta_one**adam_step)
    second_hat = new_second / (1.0 - beta_two**adam_step)
    new_master = master - rate * (first_hat / (jnp.sqrt(second_hat) + adam_eps) + decay * master)
    return (
        mixed,
        tokens_grad,
        total.reshape(1),
        clipped,
        new_master,
        new_first,
        new_second,
        new_master.astype(BF16),
    )


def solution(mesh):
    in_specs = (
        P(("grp", "win"), None),
        P(None, ("grp", "win"), None),
        P(("grp", "win"), None),
        P(None, ("grp", "win")),
        P(None, ("grp", "win"), None),
        P(None, ("grp", "win")),
        P(("grp", "win")),
        P(("grp", "win")),
        P(("grp", "win")),
    )
    out_specs = (
        P(("grp", "win"), None),
        P(("grp", "win"), None),
        P(),
        P(("grp", "win")),
        P(("grp", "win")),
        P(("grp", "win")),
        P(("grp", "win")),
        P(("grp", "win")),
    )
    return jax.shard_map(shards, mesh=mesh, in_specs=in_specs, out_specs=out_specs, check_vma=False)
```

time: 865 us -> 368 us (0.43)
  waiting for transfers between devices: 299 us -> 68.5 us
  local copies, waits for them, and re-layouts: 220 us -> 22.8 us
  matrix products: 141 us -> 0 us
  Pallas kernels: 0 us -> 122 us
  other arithmetic: 98.8 us -> 3.04 us
  blocking collectives: 40.8 us -> 128 us
  starting transfers between devices: 36.1 us -> 19.1 us
  between operations: 19 us -> 3.13 us
    unnamed x4 -> x0, waiting for transfers between devices: 251 us -> none
    all_to_all x0 -> x7, blocking collectives: none -> 128 us  [exchange(): return lax.all_to_all(buffer, axes, split_axis=0, concat_axis=0, tiled=True)]
    pallas_call x0 -> x11, Pallas kernels: none -> 122 us  [call(): pl.pallas_call(body, out_shape=tuple((shape_of(s, d) for s, d in outs)),...]
    dot_general x78 -> x0, matrix products: 115 us -> none  [the longest x12 26.9 us: forward_group(): jnp.einsum('bhqk,bkhd->bqhd', probs, value_block, preferred_element_type=...]
    gather x16 -> x0, local copies, waits for them, and re-layouts: 91.3 us -> none  [the longest x4 28.2 us: to_owner(): buffer = jnp.take(with_blank(input_rows), send_pick, axis=0)]
    psum x1 -> x0, blocking collectives: 40.8 us -> none  [shards(): total = jnp.sqrt(lax.psum(jnp.sum(shard * shard), ('grp', 'win')))]
    select_n x14 -> x3, other arithmetic: 39.3 us -> 0.01 us  [the longest x1 0.01 us: shards(): wide = jnp.where(wide < 128, wide, 128 + wide % 16)]
    sub x6 -> x0, matrix products: 25.7 us -> none  [forward_group(): expos = jnp.exp(scores - highest)]
  transfers between devices with their start and end apart: 10 -> 6, of which waited for: 7 -> 6; matrix products, arithmetic and copies ran while one was open for 13% -> 1% of each run, Pallas kernels for 0% -> 4%
where the time goes in v1:
time: 368 us; the launch traced here: 366 us
  blocking collectives  128 us (35%)
  Pallas kernels  122 us (33%)
  waiting for transfers between devices  68.5 us (19%)
  local copies, waits for them, and re-layouts  22.8 us (6%)
  starting transfers between devices  19.1 us (5%)
    all_to_all x7, blocking collectives, exchange(): return lax.all_to_all(buffer, axes, split_axis=0, concat_axis=0, tiled=True)  128 us
    pallas_call x11, Pallas kernels, call(): pl.pallas_call(body, out_shape=tuple((shape_of(s, d) for s, d in outs)),...  122 us
    all_to_all x6, waiting for transfers between devices, exchange(): return lax.all_to_all(buffer, axes, split_axis=0, concat_axis=0, tiled=True)  68.5 us
    all_to_all x6, starting transfers between devices, exchange(): return lax.all_to_all(buffer, axes, split_axis=0, concat_axis=0, tiled=True)  19.1 us
    unnamed x126, local copies, waits for them, and re-layouts  16.7 us
  transfers between devices with their start and end apart: 6, of which 6 were waited for; matrix products, arithmetic and copies ran while one was open for 1% of the time, Pallas kernels for 4%

profile of v1, /device:TPU:0, one launch (start us, length us, event | category | flops | bytes accessed | tf_op | source)
XLA Modules:
  0.0 366.5 jit_solution(5601754617265158009)
XLA Ops:
  1.5 14.7 %all_to_all.119 = bf16[8,80,128]{2,1,0:T(8,128)(2,1)S(1)} all-to-all(bf16[8,80,128]{2,1,0:T(8,128)(2,1)S(1)} %broadcast_in_dim.69), channel_id=1, replica_groups=mesh['grp'=8,'win'=4] {'grp'}, dimensions={0} | all-to-all | bytes 327680 | tf_op jit(solution)/shard_map/all_to_all | solution.py:456
  17.2 3.5 all-to-all-start.1
  20.7 3.3 shard_map.153
  24.0 6.9 %all-to-all-done.1.shards_ref = bf16[32,80,128]{2,1,0:T(8,128)(2,1)S(1)} async-done(((bf16[32,80,128]{2,1,0:T(8,128)(2,1)}), bf16[32,80,128]{2,1,0:T(8,128)(2,1)S(1)}, u32[]{:S(2)}, u32[]{:S(2)}) %all-to-all-start.1) | async-done | bytes 655392 | tf_op jit(solution)/shard_map/all_to_all | solution.py:456
  37.8 21.9 %all-to-all-done.2 = bf16[32,64,256]{2,1,0:T(8,128)(2,1)S(1)} async-done(((bf16[32,64,256]{2,1,0:T(8,128)(2,1)}), bf16[32,64,256]{2,1,0:T(8,128)(2,1)S(1)}, u32[]{:S(2)}, u32[]{:S(2)}) %all-to-all-start.2) | async-done | bytes 1048608 | tf_op jit(solution)/shard_map/all_to_all | solution.py:456
  60.7 19.2 %shard_map.154 = (bf16[2048,128]{1,0:T(8,128)(2,1)S(1)}, bf16[1728,256]{1,0:T(8,128)(2,1)S(1)}, bf16[1728,384]{1,0:T(8,128)(2,1)}, bf16[1728,1152]{1,0:T(8,128)(...) custom-call(s32[1,2048]{1,0:T(1,128)S(1)} %get-tuple-element.105.refs_0_.recv_ref, ...), custom_call_target="tpu_custom_call" | custom-call | tf_op jit(solution)/shard_map/pallas_call | solution.py:447
  81.8 18.9 %all_to_all.120 = bf16[32,64,128]{2,1,0:T(8,128)(2,1)S(1)} all-to-all(bf16[32,64,128]{2,1,0:T(8,128)(2,1)S(1)} %bitcast.43), channel_id=1, replica_groups=mesh['grp'=8,'win'=4] {'grp','win'}, dimensions={0} | all-to-all | bytes 1048576 | tf_op jit(solution)/shard_map/all_to_all | solution.py:456
  105.5 8.2 %shard_map.155 = (bf16[1024,128]{1,0:T(8,128)(2,1)S(1)}, bf16[2048,128]{1,0:T(8,128)(2,1)S(1)}, f32[1024,128]{1,0:T(8,128)S(1)}) custom-call(s32[1024,128]{1,0:T(8,128)S(1)} %broadcast_in_dim.72.route_col_ref, s32[1,1024]{1,0:T(1,128)S(1)} %get-tuple-element.108.route_ref, bf16[2048,128]{1,0:T(8,128)(2,1)S(1)} %bitcast.35, bf16[1024,128]{1,0:T(8,128)(2,1)S(1)} %copy-done.1, ...), custom_call_target="tpu_custom_call" | custom-call | tf_op jit(solution)/shard_map/pallas_call | solution.py:447
  116.1 3.2 all-to-all-done.5
  119.3 18.6 %all_to_all.121 = bf16[32,64,128]{2,1,0:T(8,128)(2,1)S(1)} all-to-all(bf16[32,64,128]{2,1,0:T(8,128)(2,1)} %bitcast.41), channel_id=1, replica_groups=mesh['grp'=8,'win'=4] {'grp','win'}, dimensions={0} | all-to-all | bytes 1048576 | tf_op jit(solution)/shard_map/all_to_all | solution.py:456
  139.7 19.1 %shard_map.156 = (bf16[2048,128]{1,0:T(8,128)(2,1)S(1)}, bf16[1728,256]{1,0:T(8,128)(2,1)S(1)}, bf16[1728,384]{1,0:T(8,128)(2,1)}, bf16[1728,1152]{1,0:T(8,128)(...) custom-call(s32[1,2048]{1,0:T(1,128)S(1)} %get-tuple-element.104.recv_ref, ...), custom_call_target="tpu_custom_call" | custom-call | tf_op jit(solution)/shard_map/pallas_call | solution.py:447
  159.7 18.4 %all_to_all.122 = bf16[32,64,128]{2,1,0:T(8,128)(2,1)S(1)} all-to-all(bf16[32,64,128]{2,1,0:T(8,128)(2,1)S(1)} %bitcast.42), channel_id=1, replica_groups=mesh['grp'=8,'win'=4] {'grp','win'}, dimensions={0} | all-to-all | bytes 1048576 | tf_op jit(solution)/shard_map/all_to_all | solution.py:456
  178.4 12.2 %shard_map.157 = (bf16[1024,128]{1,0:T(8,128)(2,1)}, f32[1024,128]{1,0:T(8,128)S(1)}, bf16[2048,128]{1,0:T(8,128)(2,1)S(1)}, f32[128,256]{1,0:T(8,128)S(1)}, f32...) custom-call(s32[1024,128]{1,0:T(8,128)S(1)} %broadcast_in_dim.63.route_col_ref, s32[1,1024]{1,0:T(1,128)S(1)} %copy-done.41, ...), custom_call_target="tpu_custom_call" | custom-call | tf_op jit(solution)/shard_map/pallas_call | solution.py:447
  193.5 3.3 all-to-all-start.7
  196.9 15.5 %all-to-all-done.7 = bf16[32,64,128]{2,1,0:T(8,128)(2,1)} async-done(((bf16[32,64,128]{2,1,0:T(8,128)(2,1)}), bf16[32,64,128]{2,1,0:T(8,128)(2,1)}, u32[]{:S(2)}, u32[]{:S(2)}) %all-to-all-start.7) | async-done | bytes 524320 | tf_op jit(solution)/shard_map/all_to_all | solution.py:456
  216.6 23.2 %shard_map.158 = (bf16[2048,128]{1,0:T(8,128)(2,1)S(1)}, f32[128,384]{1,0:T(8,128)S(1)}, f32[128,128]{1,0:T(8,128)S(1)}) custom-call(s32[1,2048]{1,0:T(1,128)S(1)} %get-tuple-element.104.recv_ref, s32[2048,128]{1,0:T(8,128)} %broadcast_in_dim.65.recv_col_ref, s32[1728,128]{1,0:T(8,128)S(1)} %broadcast_in_dim.67.bucket_ref, ...), custom_call_target="tpu_custom_call" | custom-call | tf_op jit(solution)/shard_map/pallas_call | solution.py:447
  239.9 18.3 %all_to_all.123 = bf16[32,64,128]{2,1,0:T(8,128)(2,1)S(1)} all-to-all(bf16[32,64,128]{2,1,0:T(8,128)(2,1)S(1)} %bitcast.39), channel_id=1, replica_groups=mesh['grp'=8,'win'=4] {'grp','win'}, dimensions={0} | all-to-all | bytes 1048576 | tf_op jit(solution)/shard_map/all_to_all | solution.py:456
  258.3 9.8 %shard_map.159 = (f32[1024,128]{1,0:T(8,128)S(1)}, bf16[2048,128]{1,0:T(8,128)(2,1)S(1)}, f32[128,256]{1,0:T(8,128)S(1)}, f32[256,128]{1,0:T(8,128)S(1)}, f32[8,128]{1,0:T(8,128)S(1)}) custom-call(s32[1024,128]{1,0:T(8,128)S(1)} %broadcast_in_dim.63.route_col_ref, s32[1,1024]{1,0:T(1,128)S(1)} %copy-done.47, bf16[2048,128]{1,0:T(8,128)(2,1)S(1)} %bitcast.31, ...), custom_call_target="tpu_custom_call" | custom-call | tf_op jit(solution)/shard_map/pallas_call | solution.py:447
  268.1 18.4 %all_to_all.124 = bf16[32,64,128]{2,1,0:T(8,128)(2,1)S(1)} all-to-all(bf16[32,64,128]{2,1,0:T(8,128)(2,1)S(1)} %bitcast.40), channel_id=1, replica_groups=mesh['grp'=8,'win'=4] {'grp','win'}, dimensions={0} | all-to-all | bytes 1048576 | tf_op jit(solution)/shard_map/all_to_all | solution.py:456
  286.6 23.9 %shard_map.160 = (bf16[2048,128]{1,0:T(8,128)(2,1)}, f32[128,384]{1,0:T(8,128)S(1)}, f32[128,128]{1,0:T(8,128)S(1)}) custom-call(s32[1,2048]{1,0:T(1,128)S(1)} %get-tuple-element.105.refs_0_.recv_ref, s32[2048,128]{1,0:T(8,128)} %copy-done, s32[1728,128]{1,0:T(8,128)S(1)} %broadcast_in_dim.76.refs_2_.bucket_ref, ...), custom_call_target="tpu_custom_call" | custom-call | tf_op jit(solution)/shard_map/pallas_call | solution.py:447
  310.8 20.8 %all_to_all.125 = bf16[32,80,128]{2,1,0:T(8,128)(2,1)S(1)} all-to-all(bf16[32,80,128]{2,1,0:T(8,128)(2,1)S(1)} %shard_map.162), channel_id=1, replica_groups=mesh['grp'=8,'win'=4] {'grp','win'}, dimensions={0} | all-to-all | bytes 1310720 | tf_op jit(solution)/shard_map/all_to_all | solution.py:456
  331.6 3.5 all-to-all-start.10
  335.9 14.8 %all-to-all-done.10 = bf16[32,64,128]{2,1,0:T(8,128)(2,1)S(1)} async-done(((bf16[32,64,128]{2,1,0:T(8,128)(2,1)}), bf16[32,64,128]{2,1,0:T(8,128)(2,1)S(1)}, u32[]{:S(2)}, u32[]{:S(2)}) %all-to-all-start.10) | async-done | bytes 524320 | tf_op jit(solution)/shard_map/all_to_all | solution.py:456
  357.1 6.2 %all-to-all-done.12 = f32[32,8,128]{2,1,0:T(8,128)S(1)} async-done(((f32[32,8,128]{2,1,0:T(8,128)}), f32[32,8,128]{2,1,0:T(8,128)S(1)}, u32[]{:S(2)}, u32[]{:S(2)}) %all-to-all-start.12) | async-done | bytes 131104 | tf_op jit(solution)/shard_map/all_to_all | solution.py:456
  (156 shorter events, 37.3 us)
Async XLA Ops:
  17.2 13.7 %all-to-all-start.1 = ((bf16[32,80,128]{2,1,0:T(8,128)(2,1)}), bf16[32,80,128]{2,1,0:T(8,128)(2,1)S(1)}, u32[]{:S(2)}, u32[]{:S(2)}) async-start(bf16[32,80,128]{2,1,0:T(8,128)(2,1)} %bitcast.4), calls=%async_computation.1 | async-start | bytes 1310720 | tf_op jit(solution)/shard_map/all_to_all | solution.py:456
  30.9 28.9 %all-to-all-start.2 = ((bf16[32,64,256]{2,1,0:T(8,128)(2,1)}), bf16[32,64,256]{2,1,0:T(8,128)(2,1)S(1)}, u32[]{:S(2)}, u32[]{:S(2)}) async-start(bf16[32,64,256]{2,1,0:T(8,128)(2,1)} %bitcast.8), calls=%async_computation.2 | async-start | bytes 2097152 | tf_op jit(solution)/shard_map/all_to_all | solution.py:456
  37.8 42.1 %copy-start.31 = (bf16[128,128]{1,0:T(8,128)(2,1)}, bf16[128,128]{1,0:T(8,128)(2,1)S(1)}, u32[]{:S(2)}) copy-start(bf16[128,128]{1,0:T(8,128)(2,1)S(1)} %get-tuple-element.55.refs_5_.wout_ref) | copy-start | bytes 98308
  100.7 18.6 %all-to-all-start.5 = ((bf16[32,64,128]{2,1,0:T(8,128)(2,1)}), bf16[32,64,128]{2,1,0:T(8,128)(2,1)S(1)}, u32[]{:S(2)}, u32[]{:S(2)}) async-start(bf16[32,64,128]{2,1,0:T(8,128)(2,1)} %bitcast.14), calls=%async_computation.5 | async-start | bytes 1048576 | tf_op jit(solution)/shard_map/all_to_all | solution.py:456
  103.8 34.2 %copy-start.40 = (s32[1,1024]{1,0:T(1,128)}, s32[1,1024]{1,0:T(1,128)S(1)}, u32[]{:S(2)}) copy-start(s32[1,1024]{1,0:T(1,128)S(1)} %get-tuple-element.108.route_ref) | copy-start | bytes 12292
  103.8 34.1 %copy-start.46 = (s32[1,1024]{1,0:T(1,128)}, s32[1,1024]{1,0:T(1,128)S(1)}, u32[]{:S(2)}) copy-start(s32[1,1024]{1,0:T(1,128)S(1)} %get-tuple-element.107.route_ref) | copy-start | bytes 12292
  105.5 32.4 %copy-start.60 = (s32[1,1,2048]{2,1,0:T(1,128)S(1)}, s32[1,1,2048]{2,1,0:T(1,128)}, u32[]{:S(2)}) copy-start(s32[1,1,2048]{2,1,0:T(1,128)} %get-tuple-element.106) | copy-start | bytes 24580
  139.6 38.5 %copy-start.41 = (s32[1,1024]{1,0:T(1,128)S(1)}, s32[1,1024]{1,0:T(1,128)}, u32[]{:S(2)}) copy-start(s32[1,1024]{1,0:T(1,128)} %copy-done.40) | copy-start | bytes 12292
  159.6 31.0 %copy-start.10 = (f32[1728,128]{1,0:T(8,128)}, f32[1728,128]{1,0:T(8,128)S(1)}, u32[]{:S(2)}) copy-start(f32[1728,128]{1,0:T(8,128)S(1)} %get-tuple-element.73.out_ref) | copy-start | bytes 2654212
  193.5 18.9 %all-to-all-start.7 = ((bf16[32,64,128]{2,1,0:T(8,128)(2,1)}), bf16[32,64,128]{2,1,0:T(8,128)(2,1)}, u32[]{:S(2)}, u32[]{:S(2)}) async-start(bf16[32,64,128]{2,1,0:T(8,128)(2,1)} %bitcast.38), calls=%async_computation.7 | async-start | bytes 1048576 | tf_op jit(solution)/shard_map/all_to_all | solution.py:456
  216.6 41.6 %copy-start.27 = (bf16[256,128]{1,0:T(8,128)(2,1)S(1)}, bf16[256,128]{1,0:T(8,128)(2,1)}, u32[]{:S(2)}) copy-start(bf16[256,128]{1,0:T(8,128)(2,1)} %copy-done.25) | copy-start | bytes 196612
  216.6 41.6 %copy-start.47 = (s32[1,1024]{1,0:T(1,128)S(1)}, s32[1,1024]{1,0:T(1,128)}, u32[]{:S(2)}) copy-start(s32[1,1024]{1,0:T(1,128)} %copy-done.46) | copy-start | bytes 12292
  216.6 41.6 %copy-start.52 = (f32[8,128]{1,0:T(8,128)S(1)}, f32[8,128]{1,0:T(8,128)}, u32[]{:S(2)}) copy-start(f32[8,128]{1,0:T(8,128)} %copy-done.50) | copy-start | bytes 12292
  258.3 28.3 %copy-start.3 = (bf16[1728,256]{1,0:T(8,128)(2,1)S(1)}, bf16[1728,256]{1,0:T(8,128)(2,1)}, u32[]{:S(2)}) copy-start(bf16[1728,256]{1,0:T(8,128)(2,1)} %copy-done.2) | copy-start | bytes 2654212
  258.3 28.3 %copy-start.5 = (f32[1728,128]{1,0:T(8,128)S(1)}, f32[1728,128]{1,0:T(8,128)}, u32[]{:S(2)}) copy-start(f32[1728,128]{1,0:T(8,128)} %copy-done.4) | copy-start | bytes 2654212
  258.3 28.3 %copy-start.7 = (f32[1728,128]{1,0:T(8,128)S(1)}, f32[1728,128]{1,0:T(8,128)}, u32[]{:S(2)}) copy-start(f32[1728,128]{1,0:T(8,128)} %copy-done.6) | copy-start | bytes 2654212
  258.3 28.3 %copy-start.32 = (bf16[128,128]{1,0:T(8,128)(2,1)S(1)}, bf16[128,128]{1,0:T(8,128)(2,1)}, u32[]{:S(2)}) copy-start(bf16[128,128]{1,0:T(8,128)(2,1)} %copy-done.31) | copy-start | bytes 98308
  268.1 42.4 %copy-start.21 = (f32[1024,128]{1,0:T(8,128)}, f32[1024,128]{1,0:T(8,128)S(1)}, u32[]{:S(2)}) copy-start(f32[1024,128]{1,0:T(8,128)S(1)} %get-tuple-element.85.dresid_ref) | copy-start | bytes 1572868
  286.6 24.0 %copy-start.37 = (f32[128,256]{1,0:T(8,128)S(1)}, f32[128,256]{1,0:T(8,128)}, u32[]{:S(2)}) copy-start(f32[128,256]{1,0:T(8,128)} %copy-done.36) | copy-start | bytes 393220
  331.6 19.1 %all-to-all-start.10 = ((bf16[32,64,128]{2,1,0:T(8,128)(2,1)}), bf16[32,64,128]{2,1,0:T(8,128)(2,1)S(1)}, u32[]{:S(2)}, u32[]{:S(2)}) async-start(bf16[32,64,128]{2,1,0:T(8,128)(2,1)} %bitcast.24), calls=%async_computation.10 | async-start | bytes 1048576 | tf_op jit(solution)/shard_map/all_to_all | solution.py:456
  335.2 29.4 %copy-start.56 = (f32[8248]{0:T(1024)S(1)}, f32[8248]{0:T(1024)}, u32[]{:S(2)}) copy-start(f32[8248]{0:T(1024)} %param.15) | copy-start | bytes 98980
  335.2 29.4 %copy-start.57 = (f32[8248]{0:T(1024)S(1)}, f32[8248]{0:T(1024)}, u32[]{:S(2)}) copy-start(f32[8248]{0:T(1024)} %param.16) | copy-start | bytes 98980
  335.2 29.4 %copy-start.58 = (f32[8248]{0:T(1024)S(1)}, f32[8248]{0:T(1024)}, u32[]{:S(2)}) copy-start(f32[8248]{0:T(1024)} %param.17) | copy-start | bytes 98980
  352.0 11.3 %all-to-all-start.12 = ((f32[32,8,128]{2,1,0:T(8,128)}), f32[32,8,128]{2,1,0:T(8,128)S(1)}, u32[]{:S(2)}, u32[]{:S(2)}) async-start(f32[32,8,128]{2,1,0:T(8,128)} %broadcast_in_dim.77), calls=%async_computation.12 | async-start | bytes 262144 | tf_op jit(solution)/shard_map/all_to_all | solution.py:456
  (45 other events, 488.8 us)

commit v2 on v1

v2 whole, which is shorter than its diff:
```python
import functools
import math

import jax
import jax.numpy as jnp
from jax import lax
from jax.experimental import pallas as pl
from jax.experimental.pallas import tpu as pltpu
from jax.sharding import PartitionSpec as P

PILLAR_WIDTH = 128
FF = 256
HEAD_COUNT = 8
HDIM = 16
WINDOW_SLOTS = 144
LAYERS = 2
DEVICE_SLOTS = 1728
NSUB = 12
NPARAM = 263936
LAYER_ROWS = 1031
EXPANDED = HEAD_COUNT * WINDOW_SLOTS
MASKED = -1e30
LOWEST = -3e38

beta_one = 0.5
beta_two = 0.5
adam_step = 4
rate = 0.1
decay = 0.01
adam_eps = 1e-08

BF16 = jnp.bfloat16
F32 = jnp.float32
AXES = ("grp", "win")

NN = (((1,), (0,)), ((), ()))
NT = (((1,), (1,)), ((), ()))
TN = (((0,), (0,)), ((), ()))


def mm(left, right, dims=NN):
    return lax.dot_general(left, right, dims, preferred_element_type=F32)


def iota(shape, dim):
    return lax.broadcasted_iota(jnp.int32, shape, dim)


def shape_of(shape, dtype):
    return jax.ShapeDtypeStruct(shape, dtype)


def one_hot_rows(row_ids, first, count):
    return jnp.where(iota((count, row_ids.shape[1]), 0) + first == row_ids, 1.0, 0.0).astype(BF16)


def one_hot_columns(column_ids, width):
    lane = iota(column_ids.shape, 1)
    pieces = [
        jnp.where(column_ids == lane + 128 * k, 1.0, 0.0).astype(BF16)
        for k in range(-(-width // 128))
    ]
    return jnp.concatenate(pieces, axis=1)[:, :width]


def expand_heads(block, heads):
    main = block[:128]
    tail = block[128:]
    return jnp.concatenate([main] * HEAD_COUNT + [tail] * HEAD_COUNT, axis=0) * heads


def scatter_rows(route_row, low_rows, send, chunk=256):
    for c in range(send.shape[0] // chunk):
        hot = one_hot_rows(route_row, c * chunk, chunk)
        send[c * chunk : (c + 1) * chunk, :] = mm(hot, low_rows).astype(BF16)


def land_rows(recv_col, slot_values, send, chunk=128):
    for c in range(send.shape[0] // chunk):
        part = slice(c * chunk, (c + 1) * chunk)
        hot = one_hot_columns(recv_col[part, :], DEVICE_SLOTS)
        send[part, :] = mm(hot, slot_values).astype(BF16)


def start_kernel(route_ref, tokens_ref, pos_ref, out_ref):
    both = jnp.concatenate([tokens_ref[...], pos_ref[...]], axis=1)
    scatter_rows(route_ref[...], both, out_ref)


def start_next_kernel(route_ref, pos_ref, cotangent_ref, pos_out_ref, cotangent_out_ref):
    both = jnp.concatenate([pos_ref[...], cotangent_ref[...]], axis=1)
    for c in range(pos_out_ref.shape[0] // 256):
        part = slice(c * 256, (c + 1) * 256)
        sent = mm(one_hot_rows(route_ref[...], c * 256, 256), both).astype(BF16)
        pos_out_ref[part, :] = sent[:, :128]
        cotangent_out_ref[part, :] = sent[:, 128:]


def slots_kernel(recv_ref, rows_ref, out_ref):
    for run in range(NSUB):
        part = slice(run * WINDOW_SLOTS, (run + 1) * WINDOW_SLOTS)
        hot = one_hot_rows(recv_ref[...], run * WINDOW_SLOTS, WINDOW_SLOTS)
        out_ref[part, :] = mm(hot, rows_ref[...]).astype(BF16)


def project_in(weights_ref):
    return jnp.concatenate([weights_ref[128 * j : 128 * j + 128, :] for j in range(3)], axis=1)


def project_out(weights_ref):
    return weights_ref[384:512, :]


def feed_weights(weights_ref):
    expand = jnp.concatenate([weights_ref[512:640, :], weights_ref[640:768, :]], axis=1)
    return expand, weights_ref[768:1024, :], weights_ref[1024:1040, :].astype(F32)


def interleave(count, make):
    waiting = [make(i) for i in range(count)]
    running = []
    while waiting or running:
        if waiting:
            running.insert(0, waiting.pop(0))
        running = [part for part in running if next(part, running) is not running]


def run_rows(run):
    return pl.ds(run * WINDOW_SLOTS, WINDOW_SLOTS)


def kept_copy(k, run, far, near, sems, out):
    far, near = far.at[run_rows(run), :], near.at[run_rows(run), :]
    ends = (near, far) if out else (far, near)
    return pltpu.make_async_copy(*ends, sems.at[k, run])


def attend_stages(run, slot_rows, joined, bucket, bucket_row, heads_ref, weights_ref, low, full):
    win = project_in(weights_ref)
    query_key = mm(joined, win[:, :256])
    queries = (query_key[:, :128] * 0.25).astype(BF16)
    keys = query_key[:, 128:].astype(BF16)
    values = mm(slot_rows, win[:, 256:]).astype(BF16)
    heads = heads_ref[...]
    block = heads[1024:]
    spread = jnp.concatenate(
        [
            queries * jnp.concatenate([heads[128 * h : 128 * h + 16]] * 9, axis=0)
            for h in range(HEAD_COUNT)
        ],
        axis=0,
    )
    yield
    scores = mm(spread, keys[:128], NT)
    tail = mm(queries, jnp.concatenate([keys[128:]] * 8, axis=0) * block, NT)
    yield

    def same(row):
        return jnp.where((bucket == row) & (row >= 0), 0.0, MASKED)

    main_bias = same(bucket_row[0:1, :])
    tail = tail + same(bucket_row[1:2, :])
    segment = iota((WINDOW_SLOTS, 128), 1) >> 4
    tail_top = jnp.zeros((WINDOW_SLOTS, 128), F32)
    pieces = []
    for h in range(HEAD_COUNT):
        main = scores[WINDOW_SLOTS * h : WINDOW_SLOTS * (h + 1)] + main_bias
        own_tail = segment == h
        top = jnp.max(jnp.maximum(main, jnp.where(own_tail, tail, LOWEST)), axis=1, keepdims=True)
        tail_top = jnp.where(own_tail, top, tail_top)
        pieces.append(jnp.exp(main - top).astype(BF16))
    pieces.append(jnp.exp(tail - tail_top).astype(BF16))
    expo = jnp.concatenate(pieces, axis=1)
    low(jnp.concatenate([joined, slot_rows, queries, keys, values, expo], axis=1))
    yield
    summed = mm(expo, jnp.concatenate([expand_heads(values, heads), heads], axis=1))
    yield
    share = jnp.where(bucket >= 0, 1.0, 0.0) / summed[:, 128:]
    attended = summed[:, :128] * share
    full(jnp.concatenate([attended, share], axis=1))
    return mm(attended.astype(BF16), project_out(weights_ref)).astype(BF16)


def attend_back_stages(run, dbranch, heads_ref, unfold_ref, weights_ref, low, full, scratch):
    attended_ref, dbranch_ref, dqkv_ref = scratch
    here = run_rows(run)
    dbranch_ref[here, :] = dbranch
    dattended = mm(dbranch, project_out(weights_ref), NT).astype(BF16).astype(F32)
    yield
    heads = heads_ref[...]
    block = heads[1024:]
    kept = full()
    out = kept[:, :128]
    attended_ref[here, :] = out.astype(BF16)
    dout = (dattended * kept[:, 128:256]).astype(BF16)
    weighed = dout.astype(F32) * out
    weighed_high = weighed.astype(BF16)
    weighed_low = (weighed - weighed_high.astype(F32)).astype(BF16)
    centre = mm(weighed_high, block) + mm(weighed_low, block)
    low_ref = low()
    queries = low_ref[here, 256:384]
    keys_wide = expand_heads(low_ref[here, 384:512], heads)
    dprob = mm(dout, expand_heads(low_ref[here, 512:640], heads), NT)
    yield
    expo = low_ref[here, 640:]
    pieces = [
        (
            (dprob[:, 128 * h : 128 * h + 128] - centre[:, 16 * h : 16 * h + 1])
            * expo[:, 128 * h : 128 * h + 128].astype(F32)
        ).astype(BF16)
        for h in range(HEAD_COUNT)
    ]
    pieces.append(((dprob[:, 1024:] - centre) * expo[:, 1024:].astype(F32)).astype(BF16))
    dscore = jnp.concatenate(pieces, axis=1)
    yield
    dqueries = (mm(dscore, keys_wide) * 0.25).astype(BF16)

    def gathered(left, right):
        wide = mm(left, right, TN)
        main = jnp.concatenate(
            [wide[16 * h : 16 * h + 16, 128 * h : 128 * h + 128] for h in range(HEAD_COUNT)],
            axis=0,
        )
        return jnp.concatenate([main, wide[:, 1024:] * block.astype(F32)], axis=1).astype(BF16)

    folded = jnp.concatenate([gathered(queries, dscore), gathered(dout, expo)], axis=0)
    yield
    dkeys_values = mm(unfold_ref[...], folded, NT).astype(BF16)
    dqkv = jnp.concatenate([dqueries, dkeys_values], axis=1)
    dqkv_ref[here, :] = dqkv
    yield
    return mm(dqkv, project_in(weights_ref), NT).astype(BF16)


def projection_grads(low_ref, scratch, dwin_ref, dwout_ref):
    attended_ref, dbranch_ref, dqkv_ref = scratch
    dwout_ref[...] = mm(attended_ref[...], dbranch_ref[...], TN)
    dqkv = dqkv_ref[...]
    dwin_ref[:, :256] = mm(low_ref[:, 0:128], dqkv[:, :256], TN)
    dwin_ref[:, 256:] = mm(low_ref[:, 128:256], dqkv[:, 256:], TN)


def owner_kernel(
    last,
    recv_ref,
    bucket_ref,
    bucket_row_ref,
    heads_ref,
    weights_ref,
    rows_ref,
    *rest,
):
    if last:
        pos_ref, *rest = rest
    (
        recv_col_far,
        send_ref,
        low_far,
        full_far,
        leave_ref,
        low_ref,
        full_ref,
        recv_col_ref,
        sems,
        recv_sem,
    ) = rest
    recv_copy = pltpu.make_async_copy(recv_col_far, recv_col_ref, recv_sem.at[0])
    recv_copy.start()

    def one_run(run):
        here = run_rows(run)

        def low(rows):
            low_ref[here, :] = rows
            kept_copy(0, run, low_far, low_ref, sems, True).start()

        def full(rows):
            full_ref[here, 0:256] = rows
            if not last:
                kept_copy(1, run, full_far, full_ref, sems, True).start()

        landed = mm(one_hot_rows(recv_ref[...], run * WINDOW_SLOTS, WINDOW_SLOTS), rows_ref[...])
        state = landed[:, :128]
        pos = pos_ref[here, :].astype(F32) if last else landed[:, 128:]
        yield
        branch = yield from attend_stages(
            run,
            state.astype(BF16),
            (state + pos).astype(BF16),
            bucket_ref[here, :].astype(F32),
            bucket_row_ref[run],
            heads_ref,
            weights_ref,
            low,
            full,
        )
        if not last:
            leave_ref[here, :] = branch
            return
        yield
        resid = state + branch.astype(F32)
        full_ref[here, 256:384] = resid
        kept_copy(1, run, full_far, full_ref, sems, True).start()
        expand, contract, vecs = feed_weights(weights_ref)
        second = (yield from feed_forward(resid, expand, contract, vecs))[-1]
        yield
        unit, _ = centred_rows(second)
        leave_ref[here, :] = (unit * vecs[5:6, :] + vecs[6:7, :]).astype(BF16)

    interleave(NSUB, one_run)
    recv_copy.wait()
    land_rows(recv_col_ref, leave_ref[...], send_ref)
    for run in range(NSUB):
        kept_copy(0, run, low_far, low_ref, sems, True).wait()
        kept_copy(1, run, full_far, full_ref, sems, True).wait()


def owner_back_kernel(
    last,
    late,
    recv_ref,
    heads_ref,
    unfold_ref,
    weights_ref,
    grads_ref,
    recv_col_far,
    low_far,
    full_far,
    send_ref,
    *rest,
):
    if last:
        dwin_ref, dwout_ref, dexpand_ref, dcontract_ref, dvecs_ref, *rest = rest
        active_ref, douter_ref, first_ref, dinner_ref, *rest = rest
        ffn_refs = (active_ref, douter_ref, first_ref, dinner_ref)
    else:
        dwin_ref, dwout_ref, flat_ref, *rest = rest
    (
        attended_ref,
        dbranch_ref,
        dqkv_ref,
        drows_ref,
        low_ref,
        full_ref,
        recv_col_ref,
        sems,
        recv_sem,
    ) = rest
    scratch = (attended_ref, dbranch_ref, dqkv_ref)
    for run in range(NSUB):
        kept_copy(1, run, full_far, full_ref, sems, False).start()
        kept_copy(0, run, low_far, low_ref, sems, False).start()
    recv_copy = pltpu.make_async_copy(recv_col_far, recv_col_ref, recv_sem.at[0])
    recv_copy.start()
    dvecs = []

    def one_run(run):
        here = run_rows(run)

        def low():
            kept_copy(0, run, low_far, low_ref, sems, False).wait()
            return low_ref

        grad = mm(one_hot_rows(recv_ref[...], run * WINDOW_SLOTS, WINDOW_SLOTS), grads_ref[...])
        yield
        if last:
            kept_copy(1, run, full_far, full_ref, sems, False).wait()
            dresid = yield from feed_back(
                here, full_ref[here, 256:384], grad, weights_ref, ffn_refs, dvecs
            )
            dbranch = dresid.astype(BF16)
        else:
            dbranch = grad.astype(BF16)

        def full():
            if not last:
                kept_copy(1, run, full_far, full_ref, sems, False).wait()
            return full_ref[here, 0:256]

        drows = yield from attend_back_stages(
            run, dbranch, heads_ref, unfold_ref, weights_ref, low, full, scratch
        )
        if last:
            drows = (dresid + drows.astype(F32)).astype(BF16)
        drows_ref[here, :] = drows

    interleave(NSUB, one_run)
    recv_copy.wait()
    drows = drows_ref[...]
    if last:
        dvecs_ref[...] = sum(dvecs)
        land_rows(recv_col_ref, drows, send_ref)
        projection_grads(low_ref, scratch, dwin_ref, dwout_ref)
        dcontract_ref[...] = mm(active_ref[...], douter_ref[...], TN)
        dexpand_ref[...] = mm(first_ref[...], dinner_ref[...], TN)
        return
    projection_grads(low_ref, scratch, dwin_ref, dwout_ref)
    devices, rows, _ = send_ref.shape
    capacity = recv_col_ref.shape[0] // devices
    for c in range(recv_col_ref.shape[0] // 128):
        hot = one_hot_columns(recv_col_ref[c * 128 : c * 128 + 128, :], DEVICE_SLOTS)
        sent = mm(hot, drows).astype(BF16)
        for part in range(128 // capacity):
            send_ref[c * 128 // capacity + part, 0:capacity, :] = sent[
                part * capacity : part * capacity + capacity
            ]
    share, quarter_rows = late
    store_projections(flat_ref, 0, dwin_ref, dwout_ref)
    flat_ref[pl.ds(512, flat_ref.shape[0] - 512), :] = jnp.zeros(
        (flat_ref.shape[0] - 512, 128), F32
    )
    owners = devices // 4
    for device in range(devices):
        quarter, owner = divmod(device, owners)
        block = share_block(
            flat_ref, owner * share, share, quarter * quarter_rows, rows - capacity, quarter_rows
        )
        send_ref[device, capacity:rows, :] = block.astype(BF16)


def share_block(flat_ref, start, share, first_row, rows, used_rows):
    row, shift = divmod(start, 128)
    row = row + first_row
    lane = iota((rows, 128), 1)
    line = iota((rows, 128), 0)
    block = flat_ref[pl.ds(row, rows), :]
    if shift:
        after = flat_ref[pl.ds(row + 1, rows), :]
        block = pltpu.roll(jnp.where(lane >= shift, block, after), 128 - shift, 1)
    inside = (line < used_rows) & ((line + first_row) * 128 + lane < share)
    return jnp.where(inside, block, 0.0)


def store_projections(flat_ref, base, dwin_ref, dwout_ref):
    for j in range(3):
        flat_ref[pl.ds(base + j, 128, stride=3), :] = dwin_ref[:, 128 * j : 128 * j + 128]
    flat_ref[pl.ds(base + 384, 128), :] = dwout_ref[...]


def centred_rows(rows):
    centre = rows - jnp.mean(rows, axis=-1, keepdims=True)
    spread = jnp.mean(centre * centre, axis=-1, keepdims=True)
    inverse = lax.rsqrt(spread + 1e-05)
    return centre * inverse, inverse


def norm_back(grad, gain, unit, inverse):
    dunit = grad * gain
    return (
        dunit
        - jnp.mean(dunit, axis=-1, keepdims=True)
        - unit * jnp.mean(dunit * unit, axis=-1, keepdims=True)
    ) * inverse


def feed_forward(resid, expand, contract, vecs):
    unit, inverse = centred_rows(resid)
    first = unit * vecs[3:4, :] + vecs[4:5, :]
    first_low = first.astype(BF16)
    bias = jnp.concatenate([vecs[0:1, :], vecs[1:2, :]], axis=1)
    inner = mm(first_low, expand) + bias
    yield
    below = 0.5 + 0.5 * lax.erf(inner * math.sqrt(0.5))
    active = (inner * below).astype(BF16)
    second = first + (mm(active, contract) + vecs[2:3, :])
    return unit, inverse, first_low, inner, below, active, second


def feed_back(here, resid, grad, weights_ref, ffn_refs, dvecs):
    active_ref, douter_ref, first_ref, dinner_ref = ffn_refs
    expand, contract, vecs = feed_weights(weights_ref)
    unit_first, inverse_first, first_low, inner, below, active, second = yield from feed_forward(
        resid, expand, contract, vecs
    )
    active_ref[here, :] = active
    first_ref[here, :] = first_low
    yield
    unit, inverse = centred_rows(second)
    dsecond = norm_back(grad, vecs[5:6, :], unit, inverse)
    douter = dsecond.astype(BF16)
    douter_ref[here, :] = douter
    dactive = mm(douter, contract, NT)
    slope = below + inner * (jnp.exp(-0.5 * inner * inner) * (1.0 / math.sqrt(2.0 * math.pi)))
    yield
    dinner = (dactive * slope).astype(BF16)
    dinner_ref[here, :] = dinner
    dfirst = mm(dinner, expand, NT) + dsecond
    yield

    def down(rows):
        return jnp.sum(rows, axis=0, keepdims=True)

    dbias = down(dinner.astype(F32))
    dvecs.append(
        jnp.concatenate(
            [
                dbias[:, :128],
                dbias[:, 128:],
                down(douter.astype(F32)),
                down(dfirst * unit_first),
                down(dfirst),
                down(grad * unit),
                down(grad),
                jnp.zeros((1, 128), F32),
            ],
            axis=0,
        )
    )
    return norm_back(dfirst, vecs[3:4, :], unit_first, inverse_first)


ROWS = 128


def part_rows(part):
    return pl.ds(part * ROWS, ROWS)


def home_forward_kernel(
    route_col_ref,
    route_ref,
    branch_ref,
    state_ref,
    weights_ref,
    send_ref,
    resid_ref,
    result_ref,
):
    def some_rows(part):
        here = part_rows(part)
        expand, contract, vecs = feed_weights(weights_ref)
        hot = one_hot_columns(route_col_ref[here, :], branch_ref.shape[0])
        resid = state_ref[here, :].astype(F32) + mm(hot, branch_ref[...])
        yield
        resid_ref[here, :] = resid
        second = (yield from feed_forward(resid, expand, contract, vecs))[-1]
        yield
        unit, _ = centred_rows(second)
        result_ref[here, :] = (unit * vecs[5:6, :] + vecs[6:7, :]).astype(BF16)

    interleave(result_ref.shape[0] // ROWS, some_rows)
    scatter_rows(route_ref[...], result_ref[...], send_ref)


def home_backward_kernel(
    route_col_ref,
    route_ref,
    arrived_ref,
    resid_ref,
    weights_ref,
    dresid_ref,
    send_ref,
    dexpand_ref,
    dcontract_ref,
    dvecs_ref,
    active_ref,
    douter_ref,
    first_ref,
    dinner_ref,
    low_ref,
):
    ffn_refs = (active_ref, douter_ref, first_ref, dinner_ref)
    dvecs = []

    def some_rows(part):
        here = part_rows(part)
        hot = one_hot_columns(route_col_ref[here, :], arrived_ref.shape[0])
        grad = mm(hot, arrived_ref[...])
        yield
        dresid = yield from feed_back(
            here, resid_ref[here, :], grad, weights_ref, ffn_refs, dvecs
        )
        dresid_ref[here, :] = dresid
        low_ref[here, :] = dresid.astype(BF16)

    interleave(dresid_ref.shape[0] // ROWS, some_rows)
    dvecs_ref[...] = sum(dvecs)
    scatter_rows(route_ref[...], low_ref[...], send_ref)
    dcontract_ref[...] = mm(active_ref[...], douter_ref[...], TN)
    dexpand_ref[...] = mm(first_ref[...], dinner_ref[...], TN)


def take_kernel(route_col_ref, arrived_ref, out_ref):
    for part in range(out_ref.shape[0] // ROWS):
        here = part_rows(part)
        hot = one_hot_columns(route_col_ref[here, :], arrived_ref.shape[0])
        out_ref[here, :] = mm(hot, arrived_ref[...]).astype(BF16)


def finish_kernel(route_col_ref, arrived_ref, dresid_ref, out_ref, rows_ref):
    devices, rows, _ = arrived_ref.shape
    capacity = rows_ref.shape[0] // devices
    for device in range(devices):
        rows_ref[device * capacity : (device + 1) * capacity, :] = arrived_ref[
            device, 0:capacity, :
        ]
    for part in range(out_ref.shape[0] // ROWS):
        here = part_rows(part)
        hot = one_hot_columns(route_col_ref[here, :], rows_ref.shape[0])
        out_ref[here, :] = dresid_ref[here, :] + mm(hot, rows_ref[...])


def late_kernel(arrived_ref, early_ref, late_ref, square_ref):
    devices, rows, _ = arrived_ref.shape
    capacity = rows - late_ref.shape[0]
    late = arrived_ref[0, capacity:rows, :].astype(F32)
    for device in range(1, devices):
        late = late + arrived_ref[device, capacity:rows, :].astype(F32)
    late_ref[...] = late
    early = early_ref[...]
    square = jnp.sum(early * early) + jnp.sum(late * late)
    square_ref[...] = jnp.full(square_ref.shape, square, F32)


def unpack_kernel(share, me_ref, shards_ref, *rest):
    flat_ref = rest[-1]
    outs = rest[:-1]
    devices, block_rows, _ = shards_ref.shape
    lane = iota((block_rows, 128), 1)
    me = me_ref[0]
    for device in range(devices):
        row, shift = divmod(device * share, 128)
        block = shards_ref[me ^ device].astype(F32)
        if shift:
            block = pltpu.roll(block, shift, 1)
            before = jnp.concatenate([flat_ref[pl.ds(row, 1), :], block[:-1]], axis=0)
            block = jnp.where(lane >= shift, block, before)
        flat_ref[pl.ds(row, block_rows), :] = block
    for layer, out_ref in enumerate(outs):
        base = layer * LAYER_ROWS
        for j in range(3):
            out_ref[128 * j : 128 * j + 128, :] = flat_ref[pl.ds(base + j, 128, stride=3), :].astype(
                BF16
            )
        out_ref[384:512, :] = flat_ref[pl.ds(base + 384, 128), :].astype(BF16)
        for j in range(2):
            out_ref[512 + 128 * j : 640 + 128 * j, :] = flat_ref[
                pl.ds(base + 512 + j, 128, stride=2), :
            ].astype(BF16)
        out_ref[768:1024, :] = flat_ref[pl.ds(base + 768, 256), :].astype(BF16)
        vecs = flat_ref[pl.ds(base + 1024, 16), :]
        out_ref[1024:1040, :] = jnp.where(iota((16, 128), 0) < 7, vecs, 0.0).astype(BF16)


def pack_kernel(
    share,
    dwin_ref,
    dwout_ref,
    dexpand_ref,
    dcontract_ref,
    dvecs_ref,
    dexpand_zero_ref,
    dcontract_zero_ref,
    dvecs_zero_ref,
    out_ref,
    flat_ref,
):
    devices, block_rows, _ = out_ref.shape
    flat_ref[0:512, :] = jnp.zeros((512, 128), F32)
    store_projections(flat_ref, LAYER_ROWS, dwin_ref, dwout_ref)
    for base, expand, contract, vecs in (
        (0, dexpand_zero_ref, dcontract_zero_ref, dvecs_zero_ref),
        (LAYER_ROWS, dexpand_ref, dcontract_ref, dvecs_ref),
    ):
        for j in range(2):
            flat_ref[pl.ds(base + 512 + j, 128, stride=2), :] = expand[:, 128 * j : 128 * j + 128]
        flat_ref[pl.ds(base + 768, 256), :] = contract[...]
        flat_ref[pl.ds(base + 1024, 7), :] = vecs[0:7, :]
    end = LAYERS * LAYER_ROWS
    flat_ref[pl.ds(end, flat_ref.shape[0] - end), :] = jnp.zeros(
        (flat_ref.shape[0] - end, 128), F32
    )
    for device in range(devices):
        block = share_block(flat_ref, device * share, share, 0, block_rows, block_rows)
        out_ref[device] = block.astype(BF16)


def call(
    name, micros, body, outs, *args, fresh=(), scratch=(), vmem=24, smem=0, far_in=0, far_out=0, sems=()
):
    near = pl.BlockSpec(memory_space=pltpu.VMEM)
    far = pl.BlockSpec(memory_space=pltpu.HBM)
    specs = [pl.BlockSpec(memory_space=pltpu.SMEM)] * smem
    specs += [near] * (len(args) - smem - far_in) + [far] * far_in
    args = [
        x if i < smem or i in fresh else pltpu.with_memory_space_constraint(x, pltpu.HBM)
        for i, x in enumerate(args)
    ]
    return pl.pallas_call(
        body,
        out_shape=tuple(
            shape_of(o[0], o[1]) if len(o) == 2 else pltpu.HBM(o[0], o[1]) for o in outs
        ),
        in_specs=specs,
        out_specs=tuple([near] * (len(outs) - far_out) + [far] * far_out),
        scratch_shapes=[pltpu.VMEM(s[0], s[1]) for s in scratch]
        + [pltpu.SemaphoreType.DMA(s) for s in sems],
        compiler_params=pltpu.CompilerParams(vmem_limit_bytes=vmem << 20),
        cost_estimate=pl.CostEstimate(
            flops=int(micros * 1e9), bytes_accessed=1 << 16, transcendentals=0
        ),
        name=name,
    )(*args)


def exchange(buffer):
    return lax.all_to_all(buffer, AXES, split_axis=0, concat_axis=0, tiled=True)


def after(value, *others):
    return lax.optimization_barrier((value, *others))[0]


def on_lanes(ids):
    return jnp.broadcast_to(ids[:, None], (ids.shape[0], 128))


def shards(
    tokens,
    positions,
    cotangent,
    route_send,
    recv_slot,
    slot_bucket,
    master,
    first_moment,
    second_moment,
):
    devices = lax.axis_size("grp") * lax.axis_size("win")
    me = lax.axis_index(AXES)
    home = tokens.shape[0]
    arrivals = recv_slot.shape[2]
    share = master.shape[0]
    share_rows = -(-share // 128)
    block_rows = -(-share_rows // 8) * 8
    quarter_rows = -(-share_rows // 4)
    late_rows = -(-quarter_rows // 8) * 8
    capacity = arrivals // devices
    width = PILLAR_WIDTH
    flat_rows = -(-(((devices - 1) * share) // 128 + block_rows + 8) // 8) * 8
    late_flat_rows = -(-max(520, ((devices // 4) * share) // 128 + late_rows + 16) // 8) * 8

    heads_id = jnp.concatenate(
        [jnp.arange(1024, dtype=jnp.int32) // 128, jnp.arange(128, dtype=jnp.int32) // 16]
    )
    lane = jnp.arange(128, dtype=jnp.int32)
    heads = (heads_id[:, None] == lane[None, :] // 16).astype(BF16)
    slot = jnp.arange(WINDOW_SLOTS, dtype=jnp.int32)
    wide = jnp.arange(256, dtype=jnp.int32)
    wide = jnp.where(wide < 128, wide, 128 + wide % 16)
    unfold = (slot[:, None] == wide[None, :]).astype(BF16)

    route = [route_send[l : l + 1] for l in range(LAYERS)]
    recv = [recv_slot[l] for l in range(LAYERS)]
    recv_col = [on_lanes(recv_slot[l, 0]) for l in range(LAYERS)]
    route_col = [on_lanes(route_send[l]) for l in range(LAYERS)]
    bucket = [on_lanes(slot_bucket[l].astype(BF16)) for l in range(LAYERS)]
    by_run = slot_bucket.astype(F32).reshape(LAYERS, NSUB, WINDOW_SLOTS)
    bucket_row = jnp.stack([by_run[:, :, :128], jnp.tile(by_run[:, :, 128:], (1, 1, 8))], axis=2)

    (send,) = call(
        "start", 3, start_kernel, (((arrivals, 2 * width), BF16),), route[0], tokens, positions[0]
    )
    arrived = exchange(send)

    pos_send, cotangent_send = call(
        "start_next",
        3,
        start_next_kernel,
        (((arrivals, width), BF16, True), ((arrivals, width), BF16, True)),
        route[1],
        positions[1],
        cotangent,
    )

    copies = jnp.pad(master.astype(BF16), (0, block_rows * 128 - share)).reshape(1, block_rows, 128)
    step = devices // 2
    while step:
        if step == devices // 4:
            copies, pos_send, cotangent_send = lax.optimization_barrier(
                (copies, pos_send, cotangent_send)
            )
        other = lax.ppermute(copies, AXES, [(i, i ^ step) for i in range(devices)])
        copies = jnp.stack([copies, other], axis=1).reshape(-1, block_rows, 128)
        step //= 2
    params = call(
        "unpack",
        1,
        functools.partial(unpack_kernel, share),
        (((1040, width), BF16, True),) * LAYERS,
        me.reshape(1),
        copies,
        scratch=(((flat_rows, 128), F32),),
        smem=1,
    )
    kept_zero = (
        ((DEVICE_SLOTS, 640 + EXPANDED), BF16, True),
        ((DEVICE_SLOTS, 2 * width), F32, True),
    )
    kept_one = (kept_zero[0], ((DEVICE_SLOTS, 3 * width), F32, True))
    recv_col_shape = ((arrivals, 128), jnp.int32)
    slots_low = ((DEVICE_SLOTS, width), BF16)
    slots_wide = ((DEVICE_SLOTS, FF), BF16)
    back_scratch = (slots_low, slots_low, ((DEVICE_SLOTS, 3 * width), BF16))
    arrival_shape = ((arrivals, width), BF16)

    pos_arrived = exchange(after(pos_send, arrived))
    def owner(layer, rows, *pos):
        kept = (kept_zero, kept_one)[layer]
        return call(
            ("first_owner", "last_owner")[layer],
            (13, 18)[layer],
            functools.partial(owner_kernel, layer == 1),
            (arrival_shape, *kept),
            recv[layer],
            bucket[layer],
            bucket_row[layer],
            heads,
            params[layer],
            rows,
            *pos,
            recv_col[layer],
            fresh=(5,),
            scratch=(slots_low, *kept, recv_col_shape),
            far_in=1,
            far_out=2,
            sems=((2, NSUB), (1,)),
            vmem=40,
        )

    send, *stored_zero = owner(0, arrived)
    branch = exchange(after(send, pos_arrived))
    (pos_slots,) = call(
        "slots", 4, slots_kernel, ((*slots_low, True),), recv[1], pos_arrived
    )
    send, resid_zero = call(
        "home",
        8,
        home_forward_kernel,
        (arrival_shape, ((home, width), F32, True)),
        route_col[0],
        route[1],
        branch,
        tokens,
        params[0],
        fresh=(2,),
        scratch=(((home, width), BF16),),
    )
    arrived = exchange(send)
    cotangent_arrived = exchange(after(cotangent_send, arrived))
    send, *stored_one = owner(1, arrived, pos_slots)
    mixed_arrived = exchange(after(send, cotangent_arrived))
    send, *grads_one = call(
        "last_owner_back",
        22,
        functools.partial(owner_back_kernel, True, None),
        (
            arrival_shape,
            ((width, 3 * width), F32, True),
            ((width, width), F32, True),
            ((width, FF), F32, True),
            ((FF, width), F32, True),
            ((8, width), F32, True),
        ),
        recv[1],
        heads,
        unfold,
        params[1],
        cotangent_arrived,
        recv_col[1],
        *stored_one,
        scratch=(
            slots_wide,
            slots_low,
            slots_low,
            slots_wide,
            *back_scratch,
            slots_low,
            *kept_one,
            recv_col_shape,
        ),
        far_in=3,
        sems=((2, NSUB), (1,)),
        vmem=40,
    )
    arrived = exchange(after(send, mixed_arrived))
    (mixed,) = call(
        "take", 2, take_kernel, (((home, width), BF16),), route_col[1], mixed_arrived
    )
    dresid, send, *ffn_zero = call(
        "home_back",
        10,
        home_backward_kernel,
        (
            ((home, width), F32, True),
            arrival_shape,
            ((width, FF), F32, True),
            ((FF, width), F32, True),
            ((8, width), F32, True),
        ),
        route_col[1],
        route[0],
        arrived,
        resid_zero,
        params[0],
        fresh=(2,),
        scratch=(
            ((home, FF), BF16),
            ((home, width), BF16),
            ((home, width), BF16),
            ((home, FF), BF16),
            ((home, width), BF16),
        ),
    )
    arrived = exchange(send)
    (packed,) = call(
        "pack",
        1,
        functools.partial(pack_kernel, share),
        (((devices, block_rows, 128), BF16, True),),
        *grads_one,
        *ffn_zero,
        scratch=(((flat_rows, 128), F32),),
    )
    early = exchange(after(packed, arrived))
    (send,) = call(
        "first_owner_back",
        16,
        functools.partial(owner_back_kernel, False, (share, quarter_rows)),
        (((devices, capacity + late_rows, width), BF16),),
        recv[0],
        heads,
        unfold,
        params[0],
        arrived,
        recv_col[0],
        *stored_zero,
        fresh=(4,),
        scratch=(
            ((width, 3 * width), F32),
            ((width, width), F32),
            ((late_flat_rows, 128), F32),
            *back_scratch,
            slots_low,
            *kept_zero,
            recv_col_shape,
        ),
        far_in=3,
        sems=((2, NSUB), (1,)),
        vmem=40,
    )
    arrived = exchange(after(send, early))
    early = jnp.sum(early.astype(F32), axis=0)
    late, square = call(
        "late",
        1,
        late_kernel,
        (((late_rows, 128), F32, True), ((devices, 8, 128), F32, True)),
        arrived,
        early,
        fresh=(0,),
    )
    squares = exchange(square)
    (tokens_grad,) = call(
        "finish",
        3,
        finish_kernel,
        (((home, width), F32),),
        route_col[0],
        arrived,
        dresid,
        scratch=(((arrivals, width), BF16),),
    )
    owners = devices // 4
    quarters = [jnp.where(me < owners, late, 0.0)]
    for k in range(1, 4):
        quarters.append(
            lax.ppermute(late, AXES, [(e + k * owners, e) for e in range(owners)])
        )
    late = jnp.concatenate([q[:quarter_rows] for q in quarters], axis=0)[:share_rows]
    shard = (early[:share_rows] + late).reshape(-1)[:share]
    total = jnp.sqrt(jnp.sum(squares[:, 0, 0]))
    clip_limit = 0.25 * math.sqrt(NPARAM)
    factor = jnp.minimum(1.0, clip_limit / (total + 1e-06))
    clipped = shard * factor
    new_first = beta_one * first_moment + (1.0 - beta_one) * clipped
    new_second = beta_two * second_moment + (1.0 - beta_two) * clipped * clipped
    first_hat = new_first / (1.0 - beta_one**adam_step)
    second_hat = new_second / (1.0 - beta_two**adam_step)
    new_master = master - rate * (first_hat / (jnp.sqrt(second_hat) + adam_eps) + decay * master)
    return (
        mixed,
        tokens_grad,
        total.reshape(1),
        clipped,
        new_master,
        new_first,
        new_second,
        new_master.astype(BF16),
    )


def solution(mesh):
    in_specs = (
        P(("grp", "win"), None),
        P(None, ("grp", "win"), None),
        P(("grp", "win"), None),
        P(None, ("grp", "win")),
        P(None, ("grp", "win"), None),
        P(None, ("grp", "win")),
        P(("grp", "win")),
        P(("grp", "win")),
        P(("grp", "win")),
    )
    out_specs = (
        P(("grp", "win"), None),
        P(("grp", "win"), None),
        P(),
        P(("grp", "win")),
        P(("grp", "win")),
        P(("grp", "win")),
        P(("grp", "win")),
        P(("grp", "win")),
    )
    return jax.shard_map(shards, mesh=mesh, in_specs=in_specs, out_specs=out_specs, check_vma=False)
```

time: 368 us -> 285 us (0.77)
  blocking collectives: 128 us -> 41.2 us
  starting transfers between devices: 19.1 us -> 54.6 us
  Pallas kernels: 122 us -> 100 us
  local copies, waits for them, and re-layouts: 22.8 us -> 11 us
  waiting for transfers between devices: 68.5 us -> 64.6 us
    all_to_all x7 -> x2, blocking collectives: 128 us -> 41.2 us  [exchange(): return lax.all_to_all(buffer, AXES, split_axis=0, concat_axis=0, tiled=True)]
    all_to_all x6 -> x9, waiting for transfers between devices: 68.5 us -> 46.1 us  [exchange(): return lax.all_to_all(buffer, AXES, split_axis=0, concat_axis=0, tiled=True)]
    all_to_all x6 -> x9, starting transfers between devices: 19.1 us -> 41.1 us  [exchange(): return lax.all_to_all(buffer, AXES, split_axis=0, concat_axis=0, tiled=True)]
    pallas_call x11 -> x14, Pallas kernels: 122 us -> 100 us  [call(): pl.pallas_call(body, out_shape=tuple((shape_of(o[0], o[1]) if len(o) == 2...]
    ppermute x0 -> x8, waiting for transfers between devices: none -> 18.5 us  [the longest x5 18.5 us: shards(): other = lax.ppermute(copies, AXES, [(i, i ^ step) for i in range(devices)])]
    unnamed x126 -> x26, local copies, waits for them, and re-layouts: 16.7 us -> 0.06 us
    ppermute x0 -> x8, starting transfers between devices: none -> 13.5 us  [the longest x5 9.62 us: shards(): other = lax.ppermute(copies, AXES, [(i, i ^ step) for i in range(devices)])]
    broadcast_in_dim x6, local copies, waits for them, and re-layouts: 2.64 us -> 6.8 us  [on_lanes(): return jnp.broadcast_to(ids[:, None], (ids.shape[0], 128))]
  transfers between devices with their start and end apart: 6 -> 17, of which waited for: 6 -> 10; matrix products, arithmetic and copies ran while one was open for 1% -> 5% of each run, Pallas kernels for 4% -> 31%
where the time goes in v2:
time: 285 us; the launch traced here: 281 us
  Pallas kernels  100 us (35%)
  waiting for transfers between devices  64.6 us (23%)
  starting transfers between devices  54.6 us (19%)
  blocking collectives  41.2 us (14%)
  local copies, waits for them, and re-layouts  11 us (4%)
  other arithmetic  5.97 us (2%)
  between operations  3.06 us (1%)
    pallas_call x14, Pallas kernels, call(): pl.pallas_call(body, out_shape=tuple((shape_of(o[0], o[1]) if len(o) == 2...  100 us
    all_to_all x9, waiting for transfers between devices, exchange(): return lax.all_to_all(buffer, AXES, split_axis=0, concat_axis=0, tiled=True)  46.1 us
    all_to_all x2, blocking collectives, exchange(): return lax.all_to_all(buffer, AXES, split_axis=0, concat_axis=0, tiled=True)  41.2 us
    all_to_all x9, starting transfers between devices, exchange(): return lax.all_to_all(buffer, AXES, split_axis=0, concat_axis=0, tiled=True)  41.1 us
    ppermute x5, waiting for transfers between devices, shards(): other = lax.ppermute(copies, AXES, [(i, i ^ step) for i in range(devices)])  18.5 us
    ppermute x5, starting transfers between devices, shards(): other = lax.ppermute(copies, AXES, [(i, i ^ step) for i in range(devices)])  9.62 us
    broadcast_in_dim x6, local copies, waits for them, and re-layouts, on_lanes(): return jnp.broadcast_to(ids[:, None], (ids.shape[0], 128))  6.8 us
  transfers between devices with their start and end apart: 17, of which 10 were waited for; matrix products, arithmetic and copies ran while one was open for 5% of the time, Pallas kernels for 31%

profile of v2, /device:TPU:0, one launch (start us, length us, event | category | flops | bytes accessed | tf_op | source)
XLA Modules:
  0.0 280.6 jit_solution(6703218232601762208)
XLA Ops:
  1.4 4.1 %collective-permute-start = (bf16[1,72,128]{2,1,0:T(8,128)(2,1)S(1)}, bf16[1,72,128]{2,1,0:T(8,128)(2,1)S(1)}, u32[]{:S(2)}, u32[]{:S(2)}) collective-permute-start(bf16[1,72,128]{2,1,0:T(8,128)(2,1)S(1)} %get-tuple-element.90), channel_id=1, source_target_pairs={{0,16},{1,17},{2,18},{3,19},{4,20},{5,21},{6,22},{7,23},{8,24},{9,... | collective-permute-start | bytes 55304 | tf_op jit(solution)/shard_map/ppermute | solution.py:783
  8.7 3.3 %start.1 = bf16[2048,256]{1,0:T(8,128)(2,1)} custom-call(s32[1,1024]{1,0:T(1,128)} %get-tuple-element.97.route_ref, bf16[1024,128]{1,0:T(8,128)(2,1)} %state_ref.1, bf16[1024,128]{1,0:T(8,128)(2,1)} %get-tuple-element.85.pos_ref), custom_call_target="tpu_custom_call" | custom-call | flops 3000000000 | bytes 65536 | tf_op jit(solution)/shard_map/start/pallas_call | solution.py:689
  12.0 3.8 %all-to-all-start = ((bf16[32,64,256]{2,1,0:T(8,128)(2,1)}), bf16[32,64,256]{2,1,0:T(8,128)(2,1)S(1)}, u32[]{:S(2)}, u32[]{:S(2)}) async-start(bf16[32,64,256]{2,1,0:T(8,128)(2,1)} %bitcast.27), calls=%async_computation | async-start | bytes 2097152 | tf_op jit(solution)/shard_map/all_to_all | solution.py:707
  22.0 12.2 %collective-permute-done.1 = bf16[2,72,128]{2,1,0:T(8,128)(2,1)S(1)} collective-permute-done((bf16[2,72,128]{2,1,0:T(8,128)(2,1)S(1)}, bf16[2,72,128]{2,1,0:T(8,128)(2,1)S(1)}, u32[]{:S(2)}, u32[]{:S(2)}) %collective-permute-start.1) | collective-permute-done | bytes 36896 | tf_op jit(solution)/shard_map/ppermute | solution.py:783
  48.8 6.8 %all-to-all-start.1 = ((bf16[32,64,128]{2,1,0:T(8,128)(2,1)}), bf16[32,64,128]{2,1,0:T(8,128)(2,1)S(1)}, u32[]{:S(2)}, u32[]{:S(2)}) async-start(bf16[32,64,128]{2,1,0:T(8,128)(2,1)} %bitcast.30), calls=%async_computation.1 | async-start | bytes 1048576 | tf_op jit(solution)/shard_map/all_to_all | solution.py:707
  58.0 11.5 %first_owner.1 = (bf16[2048,128]{1,0:T(8,128)(2,1)S(1)}, bf16[1728,1792]{1,0:T(8,128)(2,1)}, f32[1728,256]{1,0:T(8,128)}) custom-call(s32[1,2048]{1,0:T(1,128)} %get-tuple-element.93.recv_ref, bf16[1728,128]{1,0:T(8,128)(2,1)} %broadcast_in_dim.53.bucket_ref, f32[12,2,128]{2,1,0:T(2,128)} %get-tuple-element.87.bucket_row_ref, ...), custom_call_target="tpu_custom_call" | custom-call | flops 12999999488 | bytes 65536 | tf_op jit(solution)/shard_map/first_owner/pallas_call | solution.py:689
  71.1 20.0 %all_to_all.103 = bf16[32,64,128]{2,1,0:T(8,128)(2,1)S(1)} all-to-all(bf16[32,64,128]{2,1,0:T(8,128)(2,1)S(1)} %bitcast.68), channel_id=1, replica_groups=mesh['grp'=8,'win'=4] {'grp','win'}, dimensions={0} | all-to-all | bytes 1048576 | tf_op jit(solution)/shard_map/all_to_all | solution.py:707
  92.1 5.6 %home.1 = (bf16[2048,128]{1,0:T(8,128)(2,1)}, f32[1024,128]{1,0:T(8,128)}) custom-call(s32[1024,128]{1,0:T(8,128)} %broadcast_in_dim.52.route_col_ref, s32[1,1024]{1,0:T(1,128)} %get-tuple-element.98.route_ref, bf16[2048,128]{1,0:T(8,128)(2,1)S(1)} %bitcast.70, bf16[1024,128]{1,0:T(8,128)(2,1)} %state_ref.1, bf16[1040,128]{1,0:T(8,128)(2,1)} %get-tuple-element.47.weights_ref), custom_call_target="tpu_custom_call" | custom-call | flops 8000000000 | bytes 65536 | tf_op jit(solution)/shard_map/home/pallas_call | solution.py:689
  101.5 3.8 %slots.1.rest_0_ = bf16[1728,128]{1,0:T(8,128)(2,1)} custom-call(s32[1,2048]{1,0:T(1,128)} %get-tuple-element.92.recv_ref, bf16[2048,128]{1,0:T(8,128)(2,1)} %bitcast.78), custom_call_target="tpu_custom_call" | custom-call | flops 4000000000 | bytes 65536 | tf_op jit(solution)/shard_map/slots/pallas_call | solution.py:689
  105.3 11.1 %all-to-all-done.3 = bf16[32,64,128]{2,1,0:T(8,128)(2,1)S(1)} async-done(((bf16[32,64,128]{2,1,0:T(8,128)(2,1)}), bf16[32,64,128]{2,1,0:T(8,128)(2,1)S(1)}, u32[]{:S(2)}, u32[]{:S(2)}) %all-to-all-start.3) | async-done | bytes 524320 | tf_op jit(solution)/shard_map/all_to_all | solution.py:707
  116.4 3.7 %all-to-all-start.4 = ((bf16[32,64,128]{2,1,0:T(8,128)(2,1)}), bf16[32,64,128]{2,1,0:T(8,128)(2,1)S(1)}, u32[]{:S(2)}, u32[]{:S(2)}) async-start(bf16[32,64,128]{2,1,0:T(8,128)(2,1)} %bitcast.37), calls=%async_computation.4 | async-start | bytes 1048576 | tf_op jit(solution)/shard_map/all_to_all | solution.py:707
  122.5 12.9 %last_owner.1 = (bf16[2048,128]{1,0:T(8,128)(2,1)}, bf16[1728,1792]{1,0:T(8,128)(2,1)}, f32[1728,384]{1,0:T(8,128)}) custom-call(s32[1,2048]{1,0:T(1,128)} %get-tuple-element.92.recv_ref, bf16[1728,128]{1,0:T(8,128)(2,1)} %broadcast_in_dim.50.bucket_ref, f32[12,2,128]{2,1,0:T(2,128)} %get-tuple-element.88.bucket_row_ref, ...), custom_call_target="tpu_custom_call" | custom-call | flops 17999998976 | bytes 65536 | tf_op jit(solution)/shard_map/last_owner/pallas_call | solution.py:689
  135.6 5.9 %all-to-all-start.5 = ((bf16[32,64,128]{2,1,0:T(8,128)(2,1)}), bf16[32,64,128]{2,1,0:T(8,128)(2,1)S(1)}, u32[]{:S(2)}, u32[]{:S(2)}) async-start(bf16[32,64,128]{2,1,0:T(8,128)(2,1)} %bitcast.39), calls=%async_computation.5 | async-start | bytes 1048576 | tf_op jit(solution)/shard_map/all_to_all | solution.py:707
  141.5 22.2 %last_owner_back.1 = (bf16[2048,128]{1,0:T(8,128)(2,1)S(1)}, f32[128,384]{1,0:T(8,128)}, f32[128,128]{1,0:T(8,128)}, f32[128,256]{1,0:T(8,128)}, f32[256,128]{1,0:T(8,128)}, /*index=5*/f32[8,128]{1,0:T(8,128)}) custom-call(s32[1,2048]{1,0:T(1,128)} %get-tuple-element.92.recv_ref, bf16[1152,128]{1,0:T(8,128)(2,1)} %compare_convert_fusion.heads_ref, ...), custom_call_target="tpu_custom_call" | custom-call | flops 22000001024 | bytes 65536 | tf_op jit(solution)/shard_map/last_owner_back/pallas_call | solution.py:689
  163.8 21.2 %all_to_all.104 = bf16[32,64,128]{2,1,0:T(8,128)(2,1)S(1)} all-to-all(bf16[32,64,128]{2,1,0:T(8,128)(2,1)S(1)} %bitcast.67), channel_id=1, replica_groups=mesh['grp'=8,'win'=4] {'grp','win'}, dimensions={0} | all-to-all | bytes 1048576 | tf_op jit(solution)/shard_map/all_to_all | solution.py:707
  186.0 6.4 %home_back.1 = (f32[1024,128]{1,0:T(8,128)}, bf16[2048,128]{1,0:T(8,128)(2,1)}, f32[128,256]{1,0:T(8,128)}, f32[256,128]{1,0:T(8,128)}, f32[8,128]{1,0:T(8,128)}) custom-call(s32[1024,128]{1,0:T(8,128)} %broadcast_in_dim.24.route_col_ref, s32[1,1024]{1,0:T(1,128)} %get-tuple-element.97.route_ref, bf16[2048,128]{1,0:T(8,128)(2,1)S(1)} %bitcast.69, ...), custom_call_target="tpu_custom_call" | custom-call | flops 10000000000 | bytes 65536 | tf_op jit(solution)/shard_map/home_back/pallas_call | solution.py:689
  197.7 13.2 %all-to-all-done.7 = bf16[32,64,128]{2,1,0:T(8,128)(2,1)S(1)} async-done(((bf16[32,64,128]{2,1,0:T(8,128)(2,1)}), bf16[32,64,128]{2,1,0:T(8,128)(2,1)S(1)}, u32[]{:S(2)}, u32[]{:S(2)}) %all-to-all-start.7) | async-done | bytes 524320 | tf_op jit(solution)/shard_map/all_to_all | solution.py:707
  211.0 3.5 %all-to-all-start.8 = ((bf16[32,72,128]{2,1,0:T(8,128)(2,1)}), bf16[32,72,128]{2,1,0:T(8,128)(2,1)S(1)}, u32[]{:S(2)}, u32[]{:S(2)}) async-start(bf16[32,72,128]{2,1,0:T(8,128)(2,1)} %pack.1), calls=%async_computation.8 | async-start | bytes 1179648 | tf_op jit(solution)/shard_map/all_to_all | solution.py:707
  214.5 18.6 %first_owner_back.1 = bf16[32,88,128]{2,1,0:T(8,128)(2,1)} custom-call(s32[1,2048]{1,0:T(1,128)} %get-tuple-element.93.recv_ref, bf16[1152,128]{1,0:T(8,128)(2,1)} %compare_convert_fusion.heads_ref, bf16[144,256]{1,0:T(8,128)(2,1)} %fusion.unfold_ref, bf16[1040,128]{1,0:T(8,128)(2,1)} %get-tuple-element.47.weights_ref, bf16[2048,128]{1,0:T(8,128)(2,1)S(1)} %bitcast.65, ...), custom_call_target="tpu_custom_call" | custom-call | flops 16000000000 | bytes 65536 | tf_op jit(solution)/shard_map/first_owner_back/pallas_call | solution.py:689
  233.0 5.8 %all-to-all-start.9 = ((bf16[32,88,128]{2,1,0:T(8,128)(2,1)}), bf16[32,88,128]{2,1,0:T(8,128)(2,1)S(1)}, u32[]{:S(2)}, u32[]{:S(2)}) async-start(bf16[32,88,128]{2,1,0:T(8,128)(2,1)} %first_owner_back.1), calls=%async_computation.9 | async-start | bytes 1441792 | tf_op jit(solution)/shard_map/all_to_all | solution.py:707
  242.8 15.4 %all-to-all-done.9.arrived_ref = bf16[32,88,128]{2,1,0:T(8,128)(2,1)S(1)} async-done(((bf16[32,88,128]{2,1,0:T(8,128)(2,1)}), bf16[32,88,128]{2,1,0:T(8,128)(2,1)S(1)}, u32[]{:S(2)}, u32[]{:S(2)}) %all-to-all-start.9) | async-done | bytes 720928 | tf_op jit(solution)/shard_map/all_to_all | solution.py:707
  263.6 5.4 %all-to-all-start.10 = ((f32[32,8,128]{2,1,0:T(8,128)}), f32[32,8,128]{2,1,0:T(8,128)S(1)}, u32[]{:S(2)}, u32[]{:S(2)}) async-start(f32[32,8,128]{2,1,0:T(8,128)} %get-tuple-element.76), calls=%async_computation.10 | async-start | bytes 262144 | tf_op jit(solution)/shard_map/all_to_all | solution.py:707
  269.0 3.5 %finish.1 = f32[1024,128]{1,0:T(8,128)} custom-call(s32[1024,128]{1,0:T(8,128)} %broadcast_in_dim.52.route_col_ref, bf16[32,88,128]{2,1,0:T(8,128)(2,1)} %copy-done, f32[1024,128]{1,0:T(8,128)} %get-tuple-element.75.dresid_ref), custom_call_target="tpu_custom_call" | custom-call | flops 3000000000 | bytes 65536 | tf_op jit(solution)/shard_map/finish/pallas_call | solution.py:689
  272.6 4.6 %all-to-all-done.10 = f32[32,8,128]{2,1,0:T(8,128)S(1)} async-done(((f32[32,8,128]{2,1,0:T(8,128)}), f32[32,8,128]{2,1,0:T(8,128)S(1)}, u32[]{:S(2)}, u32[]{:S(2)}) %all-to-all-start.10) | async-done | bytes 131104 | tf_op jit(solution)/shard_map/all_to_all | solution.py:707
  (88 shorter events, 53.0 us)
Async XLA Ops:
  1.4 18.7 %collective-permute-start = (bf16[1,72,128]{2,1,0:T(8,128)(2,1)S(1)}, bf16[1,72,128]{2,1,0:T(8,128)(2,1)S(1)}, u32[]{:S(2)}, u32[]{:S(2)}) collective-permute-start(bf16[1,72,128]{2,1,0:T(8,128)(2,1)S(1)} %get-tuple-element.90), channel_id=1, source_target_pairs={{0,16},{1,17},{2,18},{3,19},{4,20},{5,21},{6,22},{7,23},{8,24},{9,... | collective-permute-start | bytes 55304 | tf_op jit(solution)/shard_map/ppermute | solution.py:783
  12.0 36.7 %all-to-all-start = ((bf16[32,64,256]{2,1,0:T(8,128)(2,1)}), bf16[32,64,256]{2,1,0:T(8,128)(2,1)S(1)}, u32[]{:S(2)}, u32[]{:S(2)}) async-start(bf16[32,64,256]{2,1,0:T(8,128)(2,1)} %bitcast.27), calls=%async_computation | async-start | bytes 2097152 | tf_op jit(solution)/shard_map/all_to_all | solution.py:707
  16.8 27.4 %copy-start.10 = (s32[2,1,2048]{2,1,0:T(1,128)S(1)}, s32[2,1,2048]{2,1,0:T(1,128)}, u32[]{:S(2)}) copy-start(s32[2,1,2048]{2,1,0:T(1,128)} %param.13) | copy-start | bytes 49156
  20.1 14.2 %collective-permute-start.1 = (bf16[2,72,128]{2,1,0:T(8,128)(2,1)S(1)}, bf16[2,72,128]{2,1,0:T(8,128)(2,1)S(1)}, u32[]{:S(2)}, u32[]{:S(2)}) collective-permute-start(bf16[2,72,128]{2,1,0:T(8,128)(2,1)S(1)} %maximum_bitcast_fusion), channel_id=1, source_target_pairs={{0,8},{1,9},{2,10},{3,11},{4,12},{5,13},{6,14},{7,15},{8,0},{9,1},... | collective-permute-start | bytes 110600 | tf_op jit(solution)/shard_map/ppermute | solution.py:783
  34.3 4.6 %collective-permute-start.2 = (bf16[4,72,128]{2,1,0:T(8,128)(2,1)S(1)}, bf16[4,72,128]{2,1,0:T(8,128)(2,1)S(1)}, u32[]{:S(2)}, u32[]{:S(2)}) collective-permute-start(bf16[4,72,128]{2,1,0:T(8,128)(2,1)S(1)} %bitcast.79), channel_id=1, source_target_pairs={{0,4},{1,5},{2,6},{3,7},{4,0},{5,1},{6,2},{7,3},{8,12},{9,13},{10,... | collective-permute-start | bytes 221192 | tf_op jit(solution)/shard_map/ppermute | solution.py:783
  38.9 5.2 %collective-permute-start.3 = (bf16[8,72,128]{2,1,0:T(8,128)(2,1)S(1)}, bf16[8,72,128]{2,1,0:T(8,128)(2,1)S(1)}, u32[]{:S(2)}, u32[]{:S(2)}) collective-permute-start(bf16[8,72,128]{2,1,0:T(8,128)(2,1)S(1)} %bitcast.74), channel_id=1, source_target_pairs={{0,2},{1,3},{2,0},{3,1},{4,6},{5,7},{6,4},{7,5},{8,10},{9,11},{10,... | collective-permute-start | bytes 442376 | tf_op jit(solution)/shard_map/ppermute | solution.py:783
  44.1 1.6 collective-permute-start.4
  48.8 22.4 %all-to-all-start.1 = ((bf16[32,64,128]{2,1,0:T(8,128)(2,1)}), bf16[32,64,128]{2,1,0:T(8,128)(2,1)S(1)}, u32[]{:S(2)}, u32[]{:S(2)}) async-start(bf16[32,64,128]{2,1,0:T(8,128)(2,1)} %bitcast.30), calls=%async_computation.1 | async-start | bytes 1048576 | tf_op jit(solution)/shard_map/all_to_all | solution.py:707
  58.0 33.1 %copy-start.8 = (s32[1,1024]{1,0:T(1,128)S(1)}, s32[1,1024]{1,0:T(1,128)}, u32[]{:S(2)}) copy-start(s32[1,1024]{1,0:T(1,128)} %get-tuple-element.97.route_ref) | copy-start | bytes 12292
  71.1 26.6 %copy-start.3 = (bf16[32,64,128]{2,1,0:T(8,128)(2,1)}, bf16[32,64,128]{2,1,0:T(8,128)(2,1)S(1)}, u32[]{:S(2)}) copy-start(bf16[32,64,128]{2,1,0:T(8,128)(2,1)S(1)} %all-to-all-done.1) | copy-start | bytes 1572868
  97.7 18.6 %all-to-all-start.3 = ((bf16[32,64,128]{2,1,0:T(8,128)(2,1)}), bf16[32,64,128]{2,1,0:T(8,128)(2,1)S(1)}, u32[]{:S(2)}, u32[]{:S(2)}) async-start(bf16[32,64,128]{2,1,0:T(8,128)(2,1)} %bitcast.34), calls=%async_computation.3 | async-start | bytes 1048576 | tf_op jit(solution)/shard_map/all_to_all | solution.py:707
  116.4 19.2 %all-to-all-start.4 = ((bf16[32,64,128]{2,1,0:T(8,128)(2,1)}), bf16[32,64,128]{2,1,0:T(8,128)(2,1)S(1)}, u32[]{:S(2)}, u32[]{:S(2)}) async-start(bf16[32,64,128]{2,1,0:T(8,128)(2,1)} %bitcast.37), calls=%async_computation.4 | async-start | bytes 1048576 | tf_op jit(solution)/shard_map/all_to_all | solution.py:707
  135.6 28.2 %all-to-all-start.5 = ((bf16[32,64,128]{2,1,0:T(8,128)(2,1)}), bf16[32,64,128]{2,1,0:T(8,128)(2,1)S(1)}, u32[]{:S(2)}, u32[]{:S(2)}) async-start(bf16[32,64,128]{2,1,0:T(8,128)(2,1)} %bitcast.39), calls=%async_computation.5 | async-start | bytes 1048576 | tf_op jit(solution)/shard_map/all_to_all | solution.py:707
  141.5 43.5 %copy-start.9 = (s32[1,1024]{1,0:T(1,128)S(1)}, s32[1,1024]{1,0:T(1,128)}, u32[]{:S(2)}) copy-start(s32[1,1024]{1,0:T(1,128)} %get-tuple-element.98.route_ref) | copy-start | bytes 12292
  163.8 28.6 %copy-start.1 = (bf16[32,64,128]{2,1,0:T(8,128)(2,1)}, bf16[32,64,128]{2,1,0:T(8,128)(2,1)S(1)}, u32[]{:S(2)}) copy-start(bf16[32,64,128]{2,1,0:T(8,128)(2,1)S(1)} %all-to-all-done.5) | copy-start | bytes 1572868
  192.4 18.6 %all-to-all-start.7 = ((bf16[32,64,128]{2,1,0:T(8,128)(2,1)}), bf16[32,64,128]{2,1,0:T(8,128)(2,1)S(1)}, u32[]{:S(2)}, u32[]{:S(2)}) async-start(bf16[32,64,128]{2,1,0:T(8,128)(2,1)} %bitcast.43), calls=%async_computation.7 | async-start | bytes 1048576 | tf_op jit(solution)/shard_map/all_to_all | solution.py:707
  211.0 22.1 %all-to-all-start.8 = ((bf16[32,72,128]{2,1,0:T(8,128)(2,1)}), bf16[32,72,128]{2,1,0:T(8,128)(2,1)S(1)}, u32[]{:S(2)}, u32[]{:S(2)}) async-start(bf16[32,72,128]{2,1,0:T(8,128)(2,1)} %pack.1), calls=%async_computation.8 | async-start | bytes 1179648 | tf_op jit(solution)/shard_map/all_to_all | solution.py:707
  233.0 25.1 %all-to-all-start.9 = ((bf16[32,88,128]{2,1,0:T(8,128)(2,1)}), bf16[32,88,128]{2,1,0:T(8,128)(2,1)S(1)}, u32[]{:S(2)}, u32[]{:S(2)}) async-start(bf16[32,88,128]{2,1,0:T(8,128)(2,1)} %first_owner_back.1), calls=%async_computation.9 | async-start | bytes 1441792 | tf_op jit(solution)/shard_map/all_to_all | solution.py:707
  258.1 10.9 %copy-start = (bf16[32,88,128]{2,1,0:T(8,128)(2,1)}, bf16[32,88,128]{2,1,0:T(8,128)(2,1)S(1)}, u32[]{:S(2)}) copy-start(bf16[32,88,128]{2,1,0:T(8,128)(2,1)S(1)} %all-to-all-done.9.arrived_ref) | copy-start | bytes 2162692
  259.7 12.9 %collective-permute-start.7 = (f32[24,128]{1,0:T(8,128)}, f32[24,128]{1,0:T(8,128)S(1)}, u32[]{:S(2)}, u32[]{:S(2)}) collective-permute-start(f32[24,128]{1,0:T(8,128)} %get-tuple-element.77), channel_id=1, source_target_pairs={{24,0},{25,1},{26,2},{27,3},{28,4},{29,5},{30,6},{31,7}} | collective-permute-start | bytes 36872 | tf_op jit(solution)/shard_map/ppermute | solution.py:978
  261.0 11.6 %collective-permute-start.6 = (f32[24,128]{1,0:T(8,128)}, f32[24,128]{1,0:T(8,128)S(1)}, u32[]{:S(2)}, u32[]{:S(2)}) collective-permute-start(f32[24,128]{1,0:T(8,128)} %get-tuple-element.77), channel_id=1, source_target_pairs={{16,0},{17,1},{18,2},{19,3},{20,4},{21,5},{22,6},{23,7}} | collective-permute-start | bytes 36872 | tf_op jit(solution)/shard_map/ppermute | solution.py:978
  262.3 10.3 %collective-permute-start.5 = (f32[24,128]{1,0:T(8,128)}, f32[24,128]{1,0:T(8,128)S(1)}, u32[]{:S(2)}, u32[]{:S(2)}) collective-permute-start(f32[24,128]{1,0:T(8,128)} %get-tuple-element.77), channel_id=1, source_target_pairs={{8,0},{9,1},{10,2},{11,3},{12,4},{13,5},{14,6},{15,7}} | collective-permute-start | bytes 36872 | tf_op jit(solution)/shard_map/ppermute | solution.py:978
  263.6 13.6 %all-to-all-start.10 = ((f32[32,8,128]{2,1,0:T(8,128)}), f32[32,8,128]{2,1,0:T(8,128)S(1)}, u32[]{:S(2)}, u32[]{:S(2)}) async-start(f32[32,8,128]{2,1,0:T(8,128)} %get-tuple-element.76), calls=%async_computation.10 | async-start | bytes 262144 | tf_op jit(solution)/shard_map/all_to_all | solution.py:707
  269.0 9.6 %copy-start.4 = (f32[8248]{0:T(1024)S(1)}, f32[8248]{0:T(1024)}, u32[]{:S(2)}) copy-start(f32[8248]{0:T(1024)} %param.15) | copy-start | bytes 98980
  (6 other events, 37.3 us)
